TPU v7x, 32 devices: a whole 2x2x4 slice. The times are simulated.
32 devices in a mesh: seq: 16 (over z, y, x), mem: 2 (over core).
Axes of the slice: x: 2, y: 2, z: 4, core: 2. Of those that a mesh axis runs over, the one named last changes fastest.
Arguments:
- tokens: bfloat16 [16384, 768], P(('seq', 'mem')), may hold values from -6 to 6
- memory: bfloat16 [4096, 768], P(('seq', 'mem')), may hold values from -6 to 6
- lengths: int32 [16], P('seq'), may hold values from 256 to 1024, as said below
- tokens_cotangent: bfloat16 [16384, 768], P(('seq', 'mem')), may hold values from -6 to 6
- memory_cotangent: bfloat16 [4096, 768], P(('seq', 'mem')), may hold values from -6 to 6
- projections: float32 [6, 768, 768], P(None, ('seq', 'mem')), may hold values from -1 to 1
- output_maps: float32 [2, 768, 768], P(None, ('seq', 'mem')), may hold values from -1 to 1
- expand_weight: float32 [768, 3072], P(('seq', 'mem')), may hold values from -0.21875 to 0.21875
- shrink_weight: float32 [3072, 768], P(('seq', 'mem')), may hold values from -0.109375 to 0.109375
- projection_bias: float32 [6, 768], P(None, ('seq', 'mem')), may hold values from -2 to 2
- norm_gain: float32 [3, 768], P(None, ('seq', 'mem')), may hold values from 0.5 to 1.5
- norm_bias: float32 [3, 768], P(None, ('seq', 'mem')), may hold values from -2 to 2
- expand_bias: float32 [3072], P(('seq', 'mem')), may hold values from -2 to 2
- shrink_bias: float32 [768], P(('seq', 'mem')), may hold values from -2 to 2
Outputs:
- new_tokens: float32 [16384, 768], P(('seq', 'mem'))
- new_memory: float32 [4096, 768], P(('seq', 'mem'))
- tokens_grad: float32 [16384, 768], P(('seq', 'mem'))
- memory_grad: float32 [4096, 768], P(('seq', 'mem'))
- projections_grad: float32 [6, 768, 768], P(None, ('seq', 'mem'))
- output_maps_grad: float32 [2, 768, 768], P(None, ('seq', 'mem'))
- expand_weight_grad: float32 [768, 3072], P(('seq', 'mem'))
- shrink_weight_grad: float32 [3072, 768], P(('seq', 'mem'))
- projection_bias_grad: float32 [6, 768], P(None, ('seq', 'mem'))
- norm_gain_grad: float32 [3, 768], P(None, ('seq', 'mem'))
- norm_bias_grad: float32 [3, 768], P(None, ('seq', 'mem'))
- expand_bias_grad: float32 [3072], P(('seq', 'mem'))
- shrink_bias_grad: float32 [768], P(('seq', 'mem'))
Inputs may be any that keep to these rules, and one draw needn't show every extreme that they name: `lengths`: every sequence has at least a quarter of its 1024 slots live; some sequence fills all 1024 in every draw; live tokens come first.
All inputs are finite; a program needn't handle non-finite values.
Results may differ from a plain program's by a relative error of at most 0.015.
Values may be sent and summed in bfloat16 or wider, within the bound.
A program may use at most 256 MiB of HBM per device.

v0:
```python
import jax
import jax.numpy as jnp
from jax import lax
from jax.sharding import PartitionSpec as P

HEADS = 12
HEAD = 64


epsilon = 1e-05


def matmul(left, right):
    return jnp.dot(left, right, preferred_element_type=jnp.float32)


def matmul_left(left, right):
    return lax.dot_general(
        left, right, (((0,), (0,)), ((), ())), preferred_element_type=jnp.float32
    )


def matmul_right(left, right):
    return lax.dot_general(
        left, right, (((1,), (1,)), ((), ())), preferred_element_type=jnp.float32
    )


def to_low(values):
    return values.astype(jnp.bfloat16)


def column_sum(values):
    return jnp.sum(values.astype(jnp.float32), axis=0)


def norm_apply(values, gain, shift):
    centre = values - jnp.mean(values, axis=-1, keepdims=True)
    spread = jnp.mean(centre * centre, axis=-1, keepdims=True)
    return centre * lax.rsqrt(spread + epsilon) * gain + shift


def gelu_exact(values):
    return jax.nn.gelu(values, approximate=False)


def score_block(queries, keys, valid):
    query_heads = queries.reshape(queries.shape[0], HEADS, HEAD)
    key_heads = keys.reshape(keys.shape[0], HEADS, HEAD)
    scores = jnp.einsum(
        "rhd,chd->hrc", query_heads, key_heads, preferred_element_type=jnp.float32
    ) * HEAD ** (-0.5)
    if valid is not None:
        scores = jnp.where(valid[None, None, :], scores, -1e30)
    return scores


def attend_forward(queries, keys, values, valid):
    scores = score_block(queries, keys, valid)
    top = jnp.max(scores, axis=-1, keepdims=True)
    expon = jnp.exp(scores - top)
    total = jnp.sum(expon, axis=-1, keepdims=True)
    probs = expon / total
    value_heads = values.reshape(values.shape[0], HEADS, HEAD)
    mixed = jnp.einsum(
        "hrc,chd->rhd", to_low(probs), value_heads, preferred_element_type=jnp.float32
    )
    mixed_float = mixed.reshape(queries.shape[0], HEADS * HEAD)
    return (to_low(mixed_float), top + jnp.log(total), mixed_float)


def attend_backward(queries, keys, values, valid, log_total, delta_mixed, row_delta):
    scores = score_block(queries, keys, valid)
    probs = jnp.exp(scores - log_total)
    count_rows = queries.shape[0]
    count_cols = keys.shape[0]
    delta_heads = delta_mixed.reshape(count_rows, HEADS, HEAD)
    value_heads = values.reshape(count_cols, HEADS, HEAD)
    query_heads = queries.reshape(count_rows, HEADS, HEAD)
    key_heads = keys.reshape(count_cols, HEADS, HEAD)
    delta_values = jnp.einsum(
        "hrc,rhd->chd", to_low(probs), delta_heads, preferred_element_type=jnp.float32
    )
    delta_probs = jnp.einsum(
        "rhd,chd->hrc", delta_heads, value_heads, preferred_element_type=jnp.float32
    )
    row_delta = jnp.sum(delta_probs * probs, axis=-1, keepdims=True)
    delta_scores = probs * (delta_probs - row_delta)
    score_low = to_low(delta_scores)
    scale = HEAD ** (-0.5)
    delta_query = (
        jnp.einsum("hrc,chd->rhd", score_low, key_heads, preferred_element_type=jnp.float32) * scale
    )
    delta_keys = (
        jnp.einsum("hrc,rhd->chd", score_low, query_heads, preferred_element_type=jnp.float32)
        * scale
    )
    return (
        delta_query.reshape(count_rows, HEADS * HEAD),
        delta_keys.reshape(count_cols, HEADS * HEAD),
        delta_values.reshape(count_cols, HEADS * HEAD),
    )


def body(
    tokens,
    memory,
    lengths,
    tokens_cotangent,
    memory_cotangent,
    projections,
    output_maps,
    expand_weight,
    shrink_weight,
    projection_bias,
    norm_gain,
    norm_bias,
    expand_bias,
    shrink_bias,
):
    gathered = (
        lax.all_gather(to_low(projections), ("seq", "mem"), axis=1, tiled=True),
        lax.all_gather(to_low(output_maps), ("seq", "mem"), axis=1, tiled=True),
        lax.all_gather(to_low(expand_weight), ("seq", "mem"), axis=0, tiled=True),
        lax.all_gather(to_low(shrink_weight), ("seq", "mem"), axis=0, tiled=True),
        lax.all_gather(to_low(projection_bias), ("seq", "mem"), axis=1, tiled=True),
        lax.all_gather(to_low(norm_gain), ("seq", "mem"), axis=1, tiled=True),
        lax.all_gather(to_low(norm_bias), ("seq", "mem"), axis=1, tiled=True),
        lax.all_gather(to_low(expand_bias), ("seq", "mem"), axis=0, tiled=True),
        lax.all_gather(to_low(shrink_bias), ("seq", "mem"), axis=0, tiled=True),
    )
    (
        proj_all,
        out_maps,
        expand_mat,
        shrink_mat,
        bias_low,
        gain_low,
        shift_low,
        expand_low,
        shrink_low,
    ) = gathered
    biases = bias_low.astype(jnp.float32)
    gains = gain_low.astype(jnp.float32)
    shifts = shift_low.astype(jnp.float32)
    expand_shift = expand_low.astype(jnp.float32)
    shrink_shift = shrink_low.astype(jnp.float32)
    tok_count = tokens.shape[0]
    share = lax.axis_index("mem")
    length = lengths[0]
    own_valid = share * tok_count + jnp.arange(tok_count) < length
    seq_count = tok_count * lax.axis_size("mem")
    all_valid = jnp.arange(seq_count) < length
    tokens_float = tokens.astype(jnp.float32)
    memory_float = memory.astype(jnp.float32)
    pack_query = to_low(matmul(memory, proj_all[0]) + biases[0])
    keys_local = to_low(matmul(tokens, proj_all[1]))
    values_local = to_low(matmul(tokens, proj_all[2]) + biases[1])
    pack_keys, pack_values = (
        lax.all_gather(keys_local, "mem", axis=0, tiled=True),
        lax.all_gather(values_local, "mem", axis=0, tiled=True),
    )
    pack_mixed, pack_total, pack_exact = attend_forward(
        pack_query, pack_keys, pack_values, all_valid
    )
    packed = matmul(pack_mixed, out_maps[0]) + biases[2]
    packed_low = to_low(packed)
    memory_sum = memory_float + packed
    new_memory = norm_apply(memory_sum, gains[0], shifts[0])
    unpack_keys_own = to_low(matmul(packed_low, proj_all[4]))
    unpack_values_own = to_low(matmul(packed_low, proj_all[5]) + biases[4])
    unpack_keys, unpack_values = (
        lax.all_gather(unpack_keys_own, "mem", axis=0, tiled=True),
        lax.all_gather(unpack_values_own, "mem", axis=0, tiled=True),
    )
    unpack_query = to_low(matmul(tokens, proj_all[3]) + biases[3])
    unpack_mixed, unpack_total, unused_exact = attend_forward(
        unpack_query, unpack_keys, unpack_values, None
    )
    unpacked = matmul(unpack_mixed, out_maps[1]) + biases[5]
    middle_sum = tokens_float + unpacked
    middle = norm_apply(middle_sum, gains[1], shifts[1])
    middle_low = to_low(middle)
    hidden_in = matmul(middle_low, expand_mat) + expand_shift
    hidden_low = to_low(gelu_exact(hidden_in))
    branch = matmul(hidden_low, shrink_mat) + shrink_shift
    output_sum = middle + branch
    layer_out = norm_apply(output_sum, gains[2], shifts[2])
    new_tokens = jnp.where(own_valid[:, None], layer_out, 0.0)
    regathered = (
        lax.all_gather(to_low(projections), ("seq", "mem"), axis=1, tiled=True),
        lax.all_gather(to_low(output_maps), ("seq", "mem"), axis=1, tiled=True),
        lax.all_gather(to_low(expand_weight), ("seq", "mem"), axis=0, tiled=True),
        lax.all_gather(to_low(shrink_weight), ("seq", "mem"), axis=0, tiled=True),
        lax.all_gather(to_low(projection_bias), ("seq", "mem"), axis=1, tiled=True),
        lax.all_gather(to_low(norm_gain), ("seq", "mem"), axis=1, tiled=True),
        lax.all_gather(to_low(norm_bias), ("seq", "mem"), axis=1, tiled=True),
        lax.all_gather(to_low(expand_bias), ("seq", "mem"), axis=0, tiled=True),
        lax.all_gather(to_low(shrink_bias), ("seq", "mem"), axis=0, tiled=True),
    )
    proj_back, maps_back, expand_back, shrink_back = (
        regathered[0],
        regathered[1],
        regathered[2],
        regathered[3],
    )
    gains_back = regathered[5].astype(jnp.float32)
    shifts_back = regathered[6].astype(jnp.float32)
    delta_out = jnp.where(own_valid[:, None], tokens_cotangent.astype(jnp.float32), 0.0)
    dropped, norm_back = jax.vjp(norm_apply, output_sum, gains_back[2], shifts_back[2])
    delta_sum2, delta_gain2, delta_shift2 = norm_back(delta_out)
    delta_branch = to_low(delta_sum2)
    delta_shrink = matmul_left(hidden_low, delta_branch)
    delta_shrink_bias = column_sum(delta_branch)
    delta_hidden = matmul_right(delta_branch, shrink_back)
    dropped, gelu_back = jax.vjp(gelu_exact, hidden_in)
    delta_hidden_in = to_low(gelu_back(delta_hidden)[0])
    delta_expand = matmul_left(middle_low, delta_hidden_in)
    delta_expand_bias = column_sum(delta_hidden_in)
    delta_middle = delta_sum2 + matmul_right(delta_hidden_in, expand_back)
    dropped, norm_back = jax.vjp(norm_apply, middle_sum, gains_back[1], shifts_back[1])
    delta_sum1, delta_gain1, delta_shift1 = norm_back(delta_middle)
    delta_unpacked = to_low(delta_sum1)
    delta_map1 = matmul_left(unpack_mixed, delta_unpacked)
    delta_bias5 = column_sum(delta_unpacked)
    delta_unpack_mixed = to_low(matmul_right(delta_unpacked, maps_back[1]))
    delta_uquery, keys_part, values_part = attend_backward(
        unpack_query, unpack_keys, unpack_values, None, unpack_total, delta_unpack_mixed, None
    )
    delta_uquery_low = to_low(delta_uquery)
    delta_proj3 = matmul_left(tokens, delta_uquery_low)
    delta_bias3 = column_sum(delta_uquery_low)
    delta_tokens = delta_sum1 + matmul_right(delta_uquery_low, proj_back[3])
    delta_ukeys, delta_uvalues = (
        lax.psum_scatter(keys_part, "mem", scatter_dimension=0, tiled=True),
        lax.psum_scatter(values_part, "mem", scatter_dimension=0, tiled=True),
    )
    delta_ukeys_low = to_low(delta_ukeys)
    delta_uvalues_low = to_low(delta_uvalues)
    delta_proj4 = matmul_left(packed_low, delta_ukeys_low)
    delta_proj5 = matmul_left(packed_low, delta_uvalues_low)
    delta_bias4 = column_sum(delta_uvalues_low)
    delta_from_keys = matmul_right(delta_ukeys_low, proj_back[4]) + matmul_right(
        delta_uvalues_low, proj_back[5]
    )
    dropped, norm_back = jax.vjp(norm_apply, memory_sum, gains_back[0], shifts_back[0])
    delta_sum0, delta_gain0, delta_shift0 = norm_back(memory_cotangent.astype(jnp.float32))
    delta_packed = to_low(delta_sum0 + delta_from_keys)
    delta_map0 = matmul_left(pack_mixed, delta_packed)
    delta_bias2 = column_sum(delta_packed)
    delta_pack_mixed = to_low(matmul_right(delta_packed, maps_back[0]))
    delta_pquery, pkeys_part, pvalues_part = attend_backward(
        pack_query, pack_keys, pack_values, all_valid, pack_total, delta_pack_mixed, None
    )
    delta_pkeys, delta_pvalues = (
        lax.psum_scatter(pkeys_part, "mem", scatter_dimension=0, tiled=True),
        lax.psum_scatter(pvalues_part, "mem", scatter_dimension=0, tiled=True),
    )
    delta_pquery_low = to_low(delta_pquery)
    delta_proj0 = matmul_left(memory, delta_pquery_low)
    delta_bias0 = column_sum(delta_pquery_low)
    memory_grad = delta_sum0 + matmul_right(delta_pquery_low, proj_back[0])
    delta_pkeys_low = to_low(delta_pkeys)
    delta_pvalues_low = to_low(delta_pvalues)
    delta_proj1 = matmul_left(tokens, delta_pkeys_low)
    delta_proj2 = matmul_left(tokens, delta_pvalues_low)
    delta_bias1 = column_sum(delta_pvalues_low)
    delta_tokens = (
        delta_tokens
        + matmul_right(delta_pkeys_low, proj_back[1])
        + matmul_right(delta_pvalues_low, proj_back[2])
    )
    grad_proj = jnp.stack(
        [delta_proj0, delta_proj1, delta_proj2, delta_proj3, delta_proj4, delta_proj5]
    )
    grad_maps = jnp.stack([delta_map0, delta_map1])
    grad_bias = jnp.stack(
        [delta_bias0, delta_bias1, delta_bias2, delta_bias3, delta_bias4, delta_bias5]
    )
    grad_gain = jnp.stack([delta_gain0, delta_gain1, delta_gain2])
    grad_shift = jnp.stack([delta_shift0, delta_shift1, delta_shift2])
    summed = (
        lax.psum_scatter(grad_proj, ("seq", "mem"), scatter_dimension=1, tiled=True),
        lax.psum_scatter(grad_maps, ("seq", "mem"), scatter_dimension=1, tiled=True),
        lax.psum_scatter(delta_expand, ("seq", "mem"), scatter_dimension=0, tiled=True),
        lax.psum_scatter(delta_shrink, ("seq", "mem"), scatter_dimension=0, tiled=True),
        lax.psum_scatter(grad_bias, ("seq", "mem"), scatter_dimension=1, tiled=True),
        lax.psum_scatter(grad_gain, ("seq", "mem"), scatter_dimension=1, tiled=True),
        lax.psum_scatter(grad_shift, ("seq", "mem"), scatter_dimension=1, tiled=True),
        lax.psum_scatter(delta_expand_bias, ("seq", "mem"), scatter_dimension=0, tiled=True),
        lax.psum_scatter(delta_shrink_bias, ("seq", "mem"), scatter_dimension=0, tiled=True),
    )
    return (
        new_tokens,
        new_memory,
        delta_tokens,
        memory_grad,
        summed[0],
        summed[1],
        summed[2],
        summed[3],
        summed[4],
        summed[5],
        summed[6],
        summed[7],
        summed[8],
    )


def solution(mesh):
    placed = (
        P(("seq", "mem"), None),
        P(("seq", "mem"), None),
        P("seq"),
        P(("seq", "mem"), None),
        P(("seq", "mem"), None),
        P(None, ("seq", "mem"), None),
        P(None, ("seq", "mem"), None),
        P(("seq", "mem"), None),
        P(("seq", "mem"), None),
        P(None, ("seq", "mem")),
        P(None, ("seq", "mem")),
        P(None, ("seq", "mem")),
        P(("seq", "mem")),
        P(("seq", "mem")),
    )
    return jax.shard_map(
        body,
        mesh=mesh,
        in_specs=placed,
        out_specs=(
            P(("seq", "mem"), None),
            P(("seq", "mem"), None),
            P(("seq", "mem"), None),
            P(("seq", "mem"), None),
            P(None, ("seq", "mem"), None),
            P(None, ("seq", "mem"), None),
            P(("seq", "mem"), None),
            P(("seq", "mem"), None),
            P(None, ("seq", "mem")),
            P(None, ("seq", "mem")),
            P(None, ("seq", "mem")),
            P(("seq", "mem")),
            P(("seq", "mem")),
        ),
        check_vma=False,
    )
```

profile of v0, /device:TPU:0, one launch (start us, length us, event | category | flops | bytes accessed | tf_op | source)
XLA Modules:
  0.0 1068.3 jit_solution(3868991310728087455)
XLA Ops:
  7.2 1.8 convert_element_type.208
  9.1 77.7 %all-gather.10.cloned.1.call-done = bf16[6,768,768]{2,1,0:T(8,128)(2,1)} async-done(((bf16[6,24,768]{2,1,0:T(8,128)(2,1)}), bf16[6,768,768]{2,1,0:T(8,128)(2,1)}) %all-gather.10.cloned.1.call-update) | async-done | bytes 7077904 | tf_op jit(solution)/shard_map/all_gather | solution.py:122
  86.8 3.2 convolution_convert_fusion.1
  90.1 39.4 %all-gather = bf16[32,24,6]{1,2,0:T(8,128)(2,1)S(1)} all-gather(bf16[1,24,6]{1,2,0:T(8,128)(2,1)S(1)} %convert_bitcast_fusion), channel_id=1, replica_groups=mesh['seq'=16,'mem'=2] {'seq','mem'}, dimensions={0}, use_global_device_ids=true | all-gather | bytes 9504 | tf_op jit(solution)/shard_map/all_gather | solution.py:126
  130.4 3.0 add_convert_fusion.2
  136.4 36.7 %all-gather.1 = bf16[32,24,3]{1,2,0:T(4,128)(2,1)S(1)} all-gather(bf16[1,24,3]{1,2,0:T(4,128)(2,1)S(1)} %convert_bitcast_fusion.2), channel_id=1, replica_groups=mesh['seq'=16,'mem'=2] {'seq','mem'}, dimensions={0}, use_global_device_ids=true | all-gather | bytes 4752 | tf_op jit(solution)/shard_map/all_gather | solution.py:127
  173.4 38.0 %all-gather.2 = bf16[32,24,3]{1,2,0:T(4,128)(2,1)S(1)} all-gather(bf16[1,24,3]{1,2,0:T(4,128)(2,1)S(1)} %convert_bitcast_fusion.1), channel_id=1, replica_groups=mesh['seq'=16,'mem'=2] {'seq','mem'}, dimensions={0}, use_global_device_ids=true | all-gather | bytes 4752 | tf_op jit(solution)/shard_map/all_gather | solution.py:128
  212.3 37.5 %all-reduce.8 = (bf16[3072]{0:T(1024)(128)(2,1)S(1)}, bf16[768]{0:T(1024)(128)(2,1)S(1)}) all-reduce(bf16[3072]{0:T(1024)(128)(2,1)S(1)} %dynamic-update-slice, bf16[768]{0:T(1024)(128)(2,1)S(1)} %dynamic-update-slice.1), channel_id=1, replica_groups=mesh['seq'=16,'mem'=2] {'seq','mem'}, use_global_device_ids=true, to_apply=%add | all-reduce | flops 3840 | bytes 15360
  252.1 1.6 fusion.25
  253.9 2.1 add_convert_fusion.1
  256.3 1.7 copy.91
  259.2 2.6 copy-done
  261.9 1.4 fusion.6
  263.4 1.7 copy.89
  265.1 5.5 fusion.28
  270.6 2.3 fusion.56
  272.9 1.7 convolution_convert_fusion.3
  274.6 2.1 all_gather.50
  276.9 1.8 fusion.26
  278.7 2.4 all_gather.49
  283.5 1.5 copy-done.1
  285.0 1.4 fusion.21
  288.8 19.7 %multiply_convert_fusion.2 = (bf16[512,3072]{1,0:T(8,128)(2,1)}, f32[512,3072]{1,0:T(8,128)}, f32[512,3072]{1,0:T(8,128)}) fusion(f32[3072]{0:T(1024)} %convert_element_type.234, bf16[768,3072]{1,0:T(8,128)(2,1)} %all-gather.18.cloned.1.call-done, f32[512,768]{1,0:T(8,128)S(1)} %get-tuple-element.118, f32[768]{0:T(1024)} %get-tuple-element.85, ...), kind=kOutput, calls=%fused_computation.10 | convolution fusion | flops 2521694208 | bytes 22042624 | tf_op jit(solution)/shard_map/dot_general | solution.py:14
  308.4 24.8 %all-gather.20.cloned.1.call-done = bf16[3072,768]{1,0:T(8,128)(2,1)} async-done(((bf16[96,768]{1,0:T(8,128)(2,1)}), bf16[3072,768]{1,0:T(8,128)(2,1)}) %all-gather.20.cloned.1.call-update) | async-done | bytes 4718608 | tf_op jit(solution)/shard_map/all_gather | solution.py:125
  333.2 6.1 fusion.60
  341.1 2.0 fusion.55
  343.9 9.1 convert_reduce_fusion
  353.0 3.6 multiply_reduce_fusion.4
  361.4 4.7 multiply_reduce_fusion.1
  366.1 1.9 multiply_convert_fusion.1
  368.1 1.7 copy-done.2
  369.8 2.0 convolution_multiply_fusion.1
  371.9 4.9 fusion.10
  379.1 2.1 fusion.31
  381.2 9.6 reduce-scatter.14.cloned.1.call-done
  390.8 2.5 convert_reduce_fusion.7
  394.0 1.8 convolution_convert_fusion.2
  396.1 4.5 multiply_reduce_fusion
  400.8 1.4 multiply_convert_fusion
  402.1 2.2 convolution_multiply_fusion
  404.5 5.8 fusion.12
  411.2 4.1 convert_reduce_fusion.3
  415.3 2.0 convert_reduce_fusion.8
  418.0 1.8 bitcast_dynamic-update-slice_fusion.3
  419.8 3.6 bitcast_dynamic-update-slice_fusion.2
  423.5 7.5 reduce-scatter.18.cloned.1.call-done
  430.9 3.6 bitcast_dynamic-update-slice_fusion.1
  434.6 2.2 bitcast_dynamic-update-slice_fusion
  436.8 2.0 bitcast_dynamic-update-slice_fusion.5
  438.7 1.9 bitcast_dynamic-update-slice_fusion.4
  440.6 17.4 %copy.107 = f32[6,768,768]{2,0,1:T(8,128)} copy(f32[6,768,768]{1,2,0:T(8,128)} %bitcast_dynamic-update-slice_fusion.4) | data formatting | bytes 28311552 | tf_op jit(solution)/shard_map/stack | solution.py:273
  460.6 2.4 pad_maximum_fusion
  464.5 7.3 fusion.49
  473.0 8.7 fusion.61
  483.9 3.5 fusion.30
  488.8 2.7 convolution_add_fusion
  492.7 42.7 %all-reduce.7 = (f32[6,768]{1,0:T(8,128)S(1)}, f32[3,768]{1,0:T(4,128)S(1)}, f32[3,768]{1,0:T(4,128)S(1)}, f32[3072]{0:T(1024)S(1)}, f32[768]{0:T(1024)S(1)}) all-reduce(f32[6,768]{1,0:T(8,128)S(1)} %stack.79, f32[3,768]{1,0:T(4,128)S(1)} %pad_maximum_fusion.1, ...), channel_id=10, replica_groups=mesh['seq'=16,'mem'=2] {'seq','mem'}, use_global_device_ids=true, to_apply=%region_32.33.clone | all-reduce | flops 13056 | bytes 104448
  538.5 2.6 fusion.29
  541.1 3.5 add_add_fusion.2
  544.6 121.8 %reduce-scatter.20.cloned.1.call-done = f32[6,24,768]{2,0,1:T(8,128)} async-done(((f32[6,768,768]{2,0,1:T(8,128)}), f32[6,24,768]{2,0,1:T(8,128)}) %reduce-scatter.20.cloned.1.call-update) | async-done | bytes 442384 | tf_op jit(solution)/shard_map/reduce_scatter | solution.py:283
  666.5 2.0 copy.108
  668.5 109.8 %reduce-scatter.22.cloned.1.call-done = f32[2,24,768]{2,1,0:T(8,128)} async-done(((f32[2,768,768]{2,1,0:T(8,128)}), f32[2,24,768]{2,1,0:T(8,128)}) %reduce-scatter.22.cloned.1.call-update) | async-done | bytes 147472 | tf_op jit(solution)/shard_map/reduce_scatter | solution.py:284
  778.3 142.1 %reduce-scatter.24.cloned.1.call-done = f32[24,3072]{1,0:T(8,128)} async-done(((f32[768,3072]{1,0:T(8,128)}), f32[24,3072]{1,0:T(8,128)}) %reduce-scatter.24.cloned.1.call-update) | async-done | bytes 294928 | tf_op jit(solution)/shard_map/reduce_scatter | solution.py:285
  920.4 141.0 %reduce-scatter.26.cloned.1.call-done = f32[96,768]{1,0:T(8,128)} async-done(((f32[3072,768]{1,0:T(8,128)}), f32[96,768]{1,0:T(8,128)}) %reduce-scatter.26.cloned.1.call-update) | async-done | bytes 294928 | tf_op jit(solution)/shard_map/reduce_scatter | solution.py:286
  (320 shorter events, 38.0 us)
Async XLA Ops:
  7.2 123.2 %copy-start.8 = (bf16[512,768]{1,0:T(8,128)(2,1)S(1)}, bf16[512,768]{1,0:T(8,128)(2,1)}, u32[]{:S(2)}) copy-start(bf16[512,768]{1,0:T(8,128)(2,1)} %param.14) | copy-start | bytes 2359300
  7.2 82.9 %copy-start.79 = (f32[6,24]{1,0:T(8,128)S(1)}, f32[6,24]{1,0:T(8,128)}, u32[]{:S(2)}) copy-start(f32[6,24]{1,0:T(8,128)} %param.23) | copy-start | bytes 1732
  7.2 79.6 %all-gather.10.cloned.1.call-start = ((), (), s32[]{:S(2)}) async-start(), calls=%async_computation.8 | async-start | bytes 7299072 | tf_op jit(solution)/shard_map/all_gather | solution.py:122
  9.1 247.3 %all-gather.14.cloned.1.call-start = ((), (), s32[]{:S(2)}) async-start(), calls=%async_computation.10 | async-start | bytes 2359296 | tf_op jit(solution)/shard_map/all_gather | solution.py:160
  90.0 43.5 %copy-start.49 = (f32[2,24,768]{2,1,0:T(8,128)S(1)}, f32[2,24,768]{2,1,0:T(8,128)}, u32[]{:S(2)}) copy-start(f32[2,24,768]{2,1,0:T(8,128)} %param.20) | copy-start | bytes 442372
  90.0 44.2 %copy-start.47 = (f32[24,3072]{1,0:T(8,128)S(1)}, f32[24,3072]{1,0:T(8,128)}, u32[]{:S(2)}) copy-start(f32[24,3072]{1,0:T(8,128)} %param.21) | copy-start | bytes 884740
  90.0 173.4 %all-gather.12.cloned.1.call-start = ((), (), s32[]{:S(2)}) async-start(), calls=%async_computation.9 | async-start | bytes 2359296 | tf_op jit(solution)/shard_map/all_gather | solution.py:161
  129.6 5.3 copy-start.48
  130.4 6.0 copy-start.84
  130.4 43.0 %copy-start.85 = (f32[3,24]{1,0:T(4,128)S(1)}, f32[3,24]{1,0:T(4,128)}, u32[]{:S(2)}) copy-start(f32[3,24]{1,0:T(4,128)} %param.25) | copy-start | bytes 868
  130.4 81.3 %copy-start.89 = (f32[96]{0:T(128)S(1)}, f32[96]{0:T(128)}, u32[]{:S(2)}) copy-start(f32[96]{0:T(128)} %param.26) | copy-start | bytes 1156
  130.4 81.4 %copy-start.90 = (f32[24]{0:T(128)S(1)}, f32[24]{0:T(128)}, u32[]{:S(2)}) copy-start(f32[24]{0:T(128)} %param.27) | copy-start | bytes 292
  130.4 121.7 %copy-start.39 = (bf16[128,768]{1,0:T(8,128)(2,1)S(1)}, bf16[128,768]{1,0:T(8,128)(2,1)}, u32[]{:S(2)}) copy-start(bf16[128,768]{1,0:T(8,128)(2,1)} %param.15) | copy-start | bytes 589828
  133.4 137.2 %all-gather.16.cloned.1.call-start = ((), (), s32[]{:S(2)}) async-start(), calls=%async_computation.11 | async-start | bytes 2433024 | tf_op jit(solution)/shard_map/all_gather | solution.py:123
  134.2 154.6 %all-gather.18.cloned.1.call-start = ((), (), s32[]{:S(2)}) async-start(), calls=%async_computation.12 | async-start | bytes 4866048 | tf_op jit(solution)/shard_map/all_gather | solution.py:124
  134.9 198.3 %all-gather.20.cloned.1.call-start = ((), (), s32[]{:S(2)}) async-start(), calls=%async_computation.13 | async-start | bytes 4866048 | tf_op jit(solution)/shard_map/all_gather | solution.py:125
  135.7 243.4 %reduce-scatter.12.cloned.1.call-start = ((), (), s32[]{:S(2)}) async-start(), calls=%async_computation.14 | async-start | bytes 1179648 | tf_op jit(solution)/shard_map/reduce_scatter | solution.py:235
  253.9 4.2 copy-start.26
  263.3 7.3 copy-start.51
  265.1 5.5 copy-start.12
  270.6 6.3 copy-start.82
  272.9 8.3 copy-start.24
  276.9 5.5 copy-start.14
  287.6 69.1 %copy-start.10 = (f32[512,768]{1,0:T(8,128)}, f32[512,768]{1,0:T(8,128)S(1)}, u32[]{:S(2)}) copy-start(f32[512,768]{1,0:T(8,128)S(1)} %get-tuple-element.118) | copy-start | bytes 4718596
  287.6 20.8 %copy-start.54 = (f32[512]{0:T(512)}, f32[512]{0:T(512)S(1)}, u32[]{:S(2)}) copy-start(f32[512]{0:T(512)S(1)} %broadcast_multiply_fusion.1) | copy-start | bytes 6148
  287.9 20.5 %copy-start.56 = (f32[512]{0:T(512)}, f32[512]{0:T(512)S(1)}, u32[]{:S(2)}) copy-start(f32[512]{0:T(512)S(1)} %multiply_reduce_fusion.8) | copy-start | bytes 6148
  288.0 20.5 %copy-start.74 = (f32[512]{0:T(512)}, f32[512]{0:T(512)S(1)}, u32[]{:S(2)}) copy-start(f32[512]{0:T(512)S(1)} %fusion.40) | copy-start | bytes 6148
  333.2 6.5 copy-start.19
  333.2 6.5 copy-start.83
  339.7 4.1 slice-start.6
  343.1 9.9 slice-start.4
  343.8 9.1 copy-start.34
  343.9 9.1 copy-start.55
  343.9 9.1 copy-start.68
  343.9 9.1 copy-start.75
  343.9 9.1 slice-start.5
  361.3 4.8 slice-start.2
  361.4 4.7 slice-start.3
  371.8 19.0 %reduce-scatter.14.cloned.1.call-start = ((), (), s32[]{:S(2)}) async-start(), calls=%async_computation.15 | async-start | bytes 1179648 | tf_op jit(solution)/shard_map/reduce_scatter | solution.py:236
  371.9 5.2 copy-start.36
  371.9 6.0 copy-start.67
  376.9 42.9 %reduce-scatter.16.cloned.1.call-start = ((), (), s32[]{:S(2)}) async-start(), calls=%async_computation.16 | async-start | bytes 4718592 | tf_op jit(solution)/shard_map/reduce_scatter | solution.py:256
  378.9 17.0 %copy-start.16 = (f32[128,768]{1,0:T(8,128)}, f32[128,768]{1,0:T(8,128)S(1)}, u32[]{:S(2)}) copy-start(f32[128,768]{1,0:T(8,128)S(1)} %get-tuple-element.100) | copy-start | bytes 1179652
  378.9 17.0 %copy-start.86 = (f32[128]{0:T(128)}, f32[128]{0:T(128)S(1)}, u32[]{:S(2)}) copy-start(f32[128]{0:T(128)S(1)} %negate_multiply_fusion.3) | copy-start | bytes 1540
  378.9 17.1 %copy-start.13 = (bf16[1024,768]{0,1:T(8,128)(2,1)S(1)}, bf16[1024,768]{0,1:T(8,128)(2,1)}, u32[]{:S(2)}) copy-start(bf16[1024,768]{0,1:T(8,128)(2,1)} %copy-done.12) | copy-start | bytes 4718596
  396.0 4.6 slice-start
  396.0 4.7 slice-start.1
  404.4 26.5 %reduce-scatter.18.cloned.1.call-start = ((), (), s32[]{:S(2)}) async-start(), calls=%async_computation.17 | async-start | bytes 4718592 | tf_op jit(solution)/shard_map/reduce_scatter | solution.py:257
  410.3 256.2 %reduce-scatter.20.cloned.1.call-start = ((), (), s32[]{:S(2)}) async-start(), calls=%async_computation.18 | async-start | bytes 19464192 | tf_op jit(solution)/shard_map/reduce_scatter | solution.py:283
  423.5 11.1 %copy-start.22 = (bf16[12,64,512]{2,1,0:T(8,128)(2,1)S(1)}, bf16[12,64,512]{2,1,0:T(8,128)(2,1)}, u32[]{:S(2)}) copy-start(bf16[12,64,512]{2,1,0:T(8,128)(2,1)} %get-tuple-element.132) | copy-start | bytes 2359300
  434.6 4.2 copy-start.18
  458.1 320.2 %reduce-scatter.22.cloned.1.call-start = ((), (), s32[]{:S(2)}) async-start(), calls=%async_computation.19 | async-start | bytes 4866048 | tf_op jit(solution)/shard_map/reduce_scatter | solution.py:284
  463.1 457.3 %reduce-scatter.24.cloned.1.call-start = ((), (), s32[]{:S(2)}) async-start(), calls=%async_computation.20 | async-start | bytes 9732096 | tf_op jit(solution)/shard_map/reduce_scatter | solution.py:285
  471.8 589.5 %reduce-scatter.26.cloned.1.call-start = ((), (), s32[]{:S(2)}) async-start(), calls=%async_computation.21 | async-start | bytes 9732096 | tf_op jit(solution)/shard_map/reduce_scatter | solution.py:286
  481.8 5.5 copy-start.53
  481.8 6.2 copy-start.66
  481.8 7.0 copy-start.17
  481.8 7.0 copy-start.29
  481.9 7.0 copy-start.87
  483.9 7.7 copy-start.7
  483.9 8.8 copy-start.60
  491.5 49.6 %copy-start.4 = (f32[512,768]{1,0:T(8,128)S(1)}, f32[512,768]{1,0:T(8,128)}, u32[]{:S(2)}) copy-start(f32[512,768]{1,0:T(8,128)} %copy-done.3) | copy-start | bytes 4718596
  491.5 49.6 %copy-start.59 = (f32[512]{0:T(512)S(1)}, f32[512]{0:T(512)}, u32[]{:S(2)}) copy-start(f32[512]{0:T(512)} %copy-done.58) | copy-start | bytes 6148
  535.3 5.8 copy-start.30
  (50 other events, 97.7 us)
Sparse Core Ops, SparseCore 0:
  11.6 75.1 all-gather.9
  90.1 8.3 all-gather.13
  133.6 5.9 all-gather.11
  142.9 58.4 all-gather.15
  204.7 62.6 all-gather.17
  270.7 62.4 all-gather.19
  372.0 7.0 reduce-scatter.11
  381.4 9.3 reduce-scatter.13
  404.5 12.0 reduce-scatter.15
  418.8 12.0 reduce-scatter.17
  458.2 208.2 reduce-scatter.19
  672.4 105.8 reduce-scatter.21
  785.8 134.5 reduce-scatter.23
  926.7 134.5 reduce-scatter.25
where the time goes:
time: 1080 us; the launch traced here: 1070 us
  waiting for transfers between devices  635 us (59%)
  blocking collectives  199 us (18%)
  matrix products  146 us (14%)
  local copies, waits for them, and re-layouts  47.7 us (4%)
  other arithmetic  23.6 us (2%)
  between operations  16.4 us (2%)
    reduce_scatter x1, waiting for transfers between devices, body(): lax.psum_scatter(delta_expand, ('seq', 'mem'), scatter_dimension=0, tiled...  142 us
    reduce_scatter x1, waiting for transfers between devices, body(): lax.psum_scatter(delta_shrink, ('seq', 'mem'), scatter_dimension=0, tiled...  141 us
    reduce_scatter x1, waiting for transfers between devices, body(): lax.psum_scatter(grad_proj, ('seq', 'mem'), scatter_dimension=1, tiled=True)  122 us
    reduce_scatter x1, waiting for transfers between devices, body(): lax.psum_scatter(grad_maps, ('seq', 'mem'), scatter_dimension=1, tiled=True)  110 us
    unnamed x2, blocking collectives  80.1 us
    all_gather x1, waiting for transfers between devices, body(): lax.all_gather(to_low(projections), ('seq', 'mem'), axis=1, tiled=True)  77.7 us
    dot_general x10, matrix products, matmul(): return jnp.dot(left, right, preferred_element_type=jnp.float32)  42.4 us
    all_gather x1, blocking collectives, body(): lax.all_gather(to_low(projection_bias), ('seq', 'mem'), axis=1, tiled=True)  39.4 us
  transfers between devices with their start and end apart: 14, of which 9 were waited for; matrix products, arithmetic and copies ran while one was open for 12% of the time, Pallas kernels for 0%

commit v1 on v0

v1 whole, which is shorter than its diff:
```python
import functools

import jax
import jax.numpy as jnp
from jax import lax
from jax.experimental import pallas as pl
from jax.experimental.pallas import tpu as pltpu
from jax.sharding import PartitionSpec as P

HEAD = 64
epsilon = 1e-05
MESH = pl.DeviceIdType.MESH
LOW = jnp.bfloat16
F32 = jnp.float32
AXES = ("seq", "mem")


def matmul(left, right):
    return jnp.dot(left, right, preferred_element_type=F32)


def matmul_left(left, right):
    return lax.dot_general(left, right, (((0,), (0,)), ((), ())), preferred_element_type=F32)


def matmul_right(left, right):
    return lax.dot_general(left, right, (((1,), (1,)), ((), ())), preferred_element_type=F32)


def to_low(values):
    return values.astype(LOW)


def column_sum(values):
    return jnp.sum(values.astype(F32), axis=0)


def swap(values):
    return lax.ppermute(values, "mem", [(0, 1), (1, 0)])


def join(own, other, axis=0):
    first = lax.axis_index("mem") == 0
    return jnp.where(
        first, jnp.concatenate([own, other], axis), jnp.concatenate([other, own], axis)
    )


def both(values, axis=0):
    return join(values, swap(values), axis)


def half(values, index, axis):
    size = values.shape[axis] // 2
    return lax.dynamic_slice_in_dim(values, index * size, size, axis)


def place(seq):
    return lax.div(seq, 4), lax.rem(lax.div(seq, 2), 2), lax.rem(seq, 2)


def peers(seq, core, far_count):
    far, row, column = place(seq)
    flat = lambda f, r, c: f * 4 + r * 2 + c
    far_peers = [lax.rem(far + k, far_count) for k in range(1, far_count)]
    return {
        "far": [(flat(f, row, column), core) for f in far_peers],
        "far_index": far_peers,
        "column": (flat(far, row, 1 - column), core),
        "row": (flat(far, 1 - row, column), core),
        "core": (seq, 1 - core),
    }


def greet(targets):
    barrier = pltpu.get_barrier_semaphore()
    for target in targets:
        pl.semaphore_signal(barrier, inc=1, device_id=target, device_id_type=MESH)
    pl.semaphore_wait(barrier, len(targets))


class Gather:
    def __init__(self, where, to, first, own, at, shared, sems):
        self.where, self.to, self.own, self.at, self.shared = where, to, own, at, shared
        self.first, self.second = first, ("row" if first == "column" else "column")
        self.send, self.recv = sems
        self.started = []

    def _column(self, near):
        far, row, column = self.where
        row, column = (
            (1 - row if "row" in near else row),
            (1 - column if "column" in near else column),
        )
        return self.at(slice(None), row, column)

    def _copy(self, source, target, k, device):
        return pltpu.make_async_remote_copy(
            source, target, self.send.at[k], self.recv.at[k], device_id=device, device_id_type=MESH
        )

    def _go(self, *args):
        copy = self._copy(*args)
        copy.start()
        self.started.append(copy)

    def _arrived(self, ref, k):
        self._copy(ref, ref, k, self.to["core"]).wait_recv()

    def start(self):
        far, row, column = self.where
        mine = self.at(far, row, column)
        for k, device in enumerate(self.to["far"]):
            self._go(self.own, mine, k, device)

    def step(self, stage):
        far, row, column = self.where
        near = self._column(())
        if stage == 0:
            count = len(self.to["far"])
            for k in range(count):
                sender = self.to["far_index"][count - 1 - k]
                self._arrived(self.at(sender, row, column), k)
            self._go(near, near, 3, self.to[self.first])
            self._go(near, near, 4, self.to[self.second])
            if self.shared:
                self._go(near, near, 6, self.to["core"])
        if stage == 1:
            got = self._column((self.first,))
            self._arrived(got, 3)
            self._go(got, got, 5, self.to[self.second])
            if self.shared:
                self._go(got, got, 7, self.to["core"])
        if stage == 2:
            for k, names in ((4, (self.second,)), (5, (self.first, self.second))):
                got = self._column(names)
                self._arrived(got, k)
                if self.shared:
                    self._go(got, got, 4 + k, self.to["core"])
        if stage == 3 and self.shared:
            for k, names in enumerate(
                ((), (self.first,), (self.second,), (self.first, self.second))
            ):
                self._arrived(self._other(names), 6 + k)

    def _other(self, names):
        keep, self.at = self.at, self.shared
        ref = self._column(names)
        self.at = keep
        return ref

    def finish(self):
        for copy in self.started:
            copy.wait_send()


def gather_kernel(far_count, proj, maps, expand, shrink, vec,
                  proj_o, maps_o, expand_o, shrink_o, vec_o, send, recv, local):
    seq, core = lax.axis_index("seq"), lax.axis_index("mem")
    where = place(seq)
    far, row, column = where
    to = peers(seq, core, far_count)
    wide = maps.shape[-1]

    def cols(which, start=0):
        return pl.ds(pl.multiple_of(which * expand.shape[-1] + start, 128), wide)

    def span(which):
        return pl.ds(pl.multiple_of(which * wide, 128), wide)

    copies = []

    def keep(source, target):
        copy = pltpu.make_async_copy(source, target, local.at[len(copies)])
        copy.start()
        copies.append(copy)

    keep(proj, proj_o.at[:, far, row, column])
    keep(maps, maps_o.at[:, far, row, column, :, span(core)])
    keep(expand, expand_o.at[far, row, column, :, pl.ds(pl.multiple_of(core * expand.shape[-1], 128), expand.shape[-1])])
    keep(shrink, shrink_o.at[far, row, column, :, span(core)])
    keep(vec, vec_o.at[far, row, column])

    units = []

    def add(first, own, at, shared):
        k = len(units)
        units.append(Gather(where, to, first, own, at, shared, (send.at[k], recv.at[k])))

    def add_proj(first, p):
        add(first, proj.at[p], lambda f, r, c: proj_o.at[p, f, r, c], None)

    def add_map(first, p):
        add(first, maps.at[p], lambda f, r, c: maps_o.at[p, f, r, c, :, span(core)],
            lambda f, r, c: maps_o.at[p, f, r, c, :, span(1 - core)])

    def add_expand(first, k):
        add(first, expand.at[:, pl.ds(k * wide, wide)], lambda f, r, c: expand_o.at[f, r, c, :, cols(core, k * wide)],
            lambda f, r, c: expand_o.at[f, r, c, :, cols(1 - core, k * wide)])

    def add_shrink(first, k):
        rows = shrink.shape[0] // 4
        part = pl.ds(k * rows, rows)
        add(first, shrink.at[part], lambda f, r, c: shrink_o.at[f, r, c, part, span(core)],
            lambda f, r, c: shrink_o.at[f, r, c, part, span(1 - core)])

    add("column", vec, lambda f, r, c: vec_o.at[f, r, c], None)
    for first, second in (
        ((add_proj, 0), (add_proj, 1)), ((add_proj, 2), (add_map, 0)), ((add_proj, 4), (add_proj, 5)), ((add_proj, 3), (add_map, 1)),
        ((add_expand, 0), (add_expand, 1)), ((add_expand, 2), (add_expand, 3)), ((add_shrink, 0), (add_shrink, 1)), ((add_shrink, 2), (add_shrink, 3)),
    ):
        first[0]("column", first[1])
        second[0]("row", second[1])

    greet(to["far"] + [to["column"], to["row"], to["core"]])
    for unit in units:
        unit.start()
    for copy in copies:
        copy.wait()
    lanes = [units[:1]] + [units[k:k + 2] for k in range(1, len(units), 2)]
    for t in range(len(lanes) + 3):
        for stage in range(4):
            if 0 <= t - stage < len(lanes):
                for unit in lanes[t - stage]:
                    unit.step(stage)
    for unit in units:
        unit.finish()


def gather_chips(far_count, blocks):
    proj, maps, expand, shrink, vec = blocks
    grid = (far_count, 2, 2)
    rows = proj.shape[1]
    shapes = (
        (6,) + grid + proj.shape[1:],
        (2,) + grid + (rows, 2 * maps.shape[2]),
        grid + (rows, 2 * expand.shape[1]),
        grid + (shrink.shape[0], 2 * shrink.shape[1]),
        grid + vec.shape,
    )
    any_space = pl.BlockSpec(memory_space=pl.ANY)
    return pl.pallas_call(
        functools.partial(gather_kernel, far_count),
        out_shape=[jax.ShapeDtypeStruct(shape, LOW) for shape in shapes],
        in_specs=[any_space] * 5,
        out_specs=[any_space] * 5,
        scratch_shapes=[
            pltpu.SemaphoreType.DMA((17, 10)),
            pltpu.SemaphoreType.DMA((17, 10)),
            pltpu.SemaphoreType.DMA((5,)),
        ],
        compiler_params=pltpu.CompilerParams(collective_id=0, has_side_effects=True),
        name="gather_weights",
    )(*blocks)


class Reduce:
    def __init__(self, where, to, first, at, total, half_in, quarter_in, far_in, sems, kind):
        self.where, self.to, self.at, self.total = where, to, at, total
        self.half_in, self.quarter_in, self.far_in, self.kind = half_in, quarter_in, far_in, kind
        self.first, self.second = first, ("row" if first == "column" else "column")
        self.send, self.recv, self.load = sems
        self.started, self.loads = [], []

    def _copy(self, source, target, k, device):
        return pltpu.make_async_remote_copy(
            source, target, self.send.at[k], self.recv.at[k], device_id=device, device_id_type=MESH
        )

    def _go(self, *args):
        copy = self._copy(*args)
        copy.start()
        self.started.append(copy)

    def _arrived(self, ref, k):
        self._copy(ref, ref, k, self.to["core"]).wait_recv()

    def _column(self, near):
        far, row, column = self.where
        row, column = (
            (1 - row if "row" in near else row),
            (1 - column if "column" in near else column),
        )
        return self.at(slice(None), row, column)

    def start(self):
        for k, names in enumerate(((self.second,), (self.first, self.second))):
            self._go(self._column(names), self.half_in.at[k], k, self.to[self.second])
        for k, names in enumerate(((), (self.first,))):
            copy = pltpu.make_async_copy(self._column(names), self.total.at[k], self.load.at[k])
            copy.start()
            self.loads.append(copy)

    def _add(self, target, other):
        count = target.shape[0]
        for k in range(count):
            target[k] = (target[k].astype(F32) + other[k].astype(F32)).astype(self.kind)

    def step(self, stage):
        count = len(self.to["far"])
        if stage == 0:
            self.loads[1].wait()
            self._arrived(self.half_in.at[1], 1)
            self._add(self.total.at[1], self.half_in.at[1])
            self._go(self.total.at[1], self.quarter_in, 2, self.to[self.first])
            self.loads[0].wait()
            self._arrived(self.half_in.at[0], 0)
            self._add(self.total.at[0], self.half_in.at[0])
        if stage == 1:
            self._arrived(self.quarter_in, 2)
            self._add(self.total.at[0], self.quarter_in)
            for k, device in enumerate(self.to["far"]):
                self._go(self.total.at[0, self.to["far_index"][k]], self.far_in.at[k], 3 + k, device)
        if stage == 2:
            for k in range(count):
                self._arrived(self.far_in.at[k], 3 + k)

    def result(self):
        value = self.total[0, self.where[0]].astype(F32)
        for k in range(len(self.to["far"])):
            value = value + self.far_in[k].astype(F32)
        return value

    def finish(self):
        for copy in self.started:
            copy.wait_send()


def reduce_kernel(far_count, proj, maps, expand, shrink, vec,
                  proj_o, maps_o, expand_o, shrink_o, vec_o,
                  total, half_in, quarter_in, far_in, vtotal, vhalf, vquarter, vfar, sums, vsum, vother,
                  send, recv, load, last_send, last_recv, last_local):
    seq, core = lax.axis_index("seq"), lax.axis_index("mem")
    where = place(seq)
    to = peers(seq, core, far_count)
    wide = maps.shape[-1]
    rows = proj.shape[-2]
    part = rows // 2
    units, ends = [], []

    def span(which, start=0, whole=None):
        return pl.ds(pl.multiple_of(which * (whole or wide) + start, 128), wide)

    def add(at, end):
        k = len(units)
        first = "column" if k % 2 == 0 else "row"
        units.append(Reduce(where, to, first, at, total.at[k], half_in.at[k], quarter_in.at[k], far_in.at[k],
                            (send.at[k], recv.at[k], load.at[k]), LOW))
        ends.append(end)

    def add_expand(k):
        add(lambda f, r, c: expand.at[f, r, c, :, pl.ds(k * wide, wide)],
            lambda which: expand_o.at[:, span(which, k * wide, expand.shape[-1])])

    def add_shrink(k):
        add(lambda f, r, c: shrink.at[f, r, c, pl.ds(k * rows, rows)], None)

    def add_map(p):
        add(lambda f, r, c: maps.at[p, f, r, c], lambda which: maps_o.at[p, :, span(which)])

    def add_proj(p):
        add(lambda f, r, c: proj.at[p, f, r, c], lambda which: proj_o.at[p, :, span(which)])

    for k in range(4):
        add_shrink(k)
    for k in range(4):
        add_expand(k)
    for make, p in ((add_map, 1), (add_proj, 3), (add_proj, 4), (add_proj, 5), (add_map, 0), (add_proj, 0), (add_proj, 1), (add_proj, 2)):
        make(p)
    vectors = Reduce(where, to, "column", lambda f, r, c: vec.at[f, r, c], vtotal, vhalf, vquarter, vfar,
                     (send.at[16], recv.at[16], load.at[16]), F32)

    greet(to["far"] + [to["column"], to["row"], to["core"]])
    order = units + [vectors]
    for unit in order:
        unit.start()
    lanes = [units[k:k + 2] for k in range(0, 16, 2)]
    lanes[0] = [vectors] + lanes[0]
    final = []
    index = {id(unit): k for k, unit in enumerate(units)}

    def close(unit):
        if unit is vectors:
            vsum[...] = vectors.result()
            mine, other = pl.ds(pl.multiple_of(core * 8, 8), 8), pl.ds(pl.multiple_of((1 - core) * 8, 8), 8)
            copy = pltpu.make_async_remote_copy(vsum.at[other], vother, last_send.at[16], last_recv.at[16],
                                                device_id=to["core"], device_id_type=MESH)
            copy.start()
            final.append(copy)
            return
        k = index[id(unit)]
        sums[k] = unit.result()
        if ends[k] is None:
            low = part * 4
            owner = k // 2
            row = pl.ds((k % 2) * rows, rows)

            @pl.when(core == owner)
            def _():
                local = pltpu.make_async_copy(sums.at[k], shrink_o.at[row, span(core)], last_local.at[k])
                local.start()
                local.wait()
                pltpu.make_async_remote_copy(sums.at[k], shrink_o.at[row, span(1 - core)], last_send.at[k], last_recv.at[k],
                                             device_id=to["core"], device_id_type=MESH).wait_recv()

            @pl.when(core != owner)
            def _():
                copy = pltpu.make_async_remote_copy(sums.at[k], shrink_o.at[row, span(core)], last_send.at[k], last_recv.at[k],
                                                    device_id=to["core"], device_id_type=MESH)
                copy.start()
                copy.wait_send()
            return
        mine = sums.at[k, pl.ds(pl.multiple_of(core * part, 8), part)]
        other = sums.at[k, pl.ds(pl.multiple_of((1 - core) * part, 8), part)]
        local = pltpu.make_async_copy(mine, ends[k](core), last_local.at[k])
        local.start()
        copy = pltpu.make_async_remote_copy(other, ends[k](core), last_send.at[k], last_recv.at[k],
                                            device_id=to["core"], device_id_type=MESH)
        copy.start()
        final.append((local, copy, ends[k](1 - core), k))

    for t in range(len(lanes) + 2):
        for stage in range(3):
            if 0 <= t - stage < len(lanes):
                for unit in lanes[t - stage]:
                    unit.step(stage)
                    if stage == 2:
                        close(unit)
    for item in final:
        if not isinstance(item, tuple):
            item.wait()
            vec_o[...] = vsum[pl.ds(pl.multiple_of(core * 8, 8), 8)] + vother[...]
        else:
            local, copy, ref, k = item
            local.wait()
            copy.wait_send()
            pltpu.make_async_remote_copy(ref, ref, last_send.at[k], last_recv.at[k],
                                         device_id=to["core"], device_id_type=MESH).wait_recv()
    for unit in order:
        unit.finish()


def reduce_chips(far_count, grads):
    proj, maps, expand, shrink, vec = grads
    rows, wide = proj.shape[-2], proj.shape[-1]
    part = rows // 2
    any_space = pl.BlockSpec(memory_space=pl.ANY)
    vmem = pl.BlockSpec(memory_space=pltpu.VMEM)
    shapes = ((6, part, 2 * wide), (2, part, 2 * wide), (part, 8 * wide), (4 * part, 2 * wide), (8, 128))
    return pl.pallas_call(
        functools.partial(reduce_kernel, far_count),
        out_shape=[jax.ShapeDtypeStruct(shape, F32) for shape in shapes],
        in_specs=[any_space] * 5,
        out_specs=[vmem] * 5,
        scratch_shapes=[
            pltpu.VMEM((16, 2, far_count, rows, wide), LOW),
            pltpu.VMEM((16, 2, far_count, rows, wide), LOW),
            pltpu.VMEM((16, far_count, rows, wide), LOW),
            pltpu.VMEM((16, far_count - 1, rows, wide), LOW),
            pltpu.VMEM((2, far_count, 16, 128), F32),
            pltpu.VMEM((2, far_count, 16, 128), F32),
            pltpu.VMEM((far_count, 16, 128), F32),
            pltpu.VMEM((far_count - 1, 16, 128), F32),
            pltpu.VMEM((16, rows, wide), F32),
            pltpu.VMEM((16, 128), F32),
            pltpu.VMEM((8, 128), F32),
            pltpu.SemaphoreType.DMA((17, 6)),
            pltpu.SemaphoreType.DMA((17, 6)),
            pltpu.SemaphoreType.DMA((17, 2)),
            pltpu.SemaphoreType.DMA((17,)),
            pltpu.SemaphoreType.DMA((17,)),
            pltpu.SemaphoreType.DMA((17,)),
        ],
        compiler_params=pltpu.CompilerParams(
            collective_id=1, has_side_effects=True, vmem_limit_bytes=48 << 20
        ),
        name="sum_gradients",
    )(*grads)


def norm_apply(values, gain, shift):
    centre = values - jnp.mean(values, axis=-1, keepdims=True)
    spread = jnp.mean(centre * centre, axis=-1, keepdims=True)
    return centre * lax.rsqrt(spread + epsilon) * gain + shift


def gelu_exact(values):
    return jax.nn.gelu(values, approximate=False)


def heads_of(values):
    return values.reshape(values.shape[0], values.shape[1] // HEAD, HEAD)


def scores_of(queries, keys, valid):
    scores = jnp.einsum(
        "rhd,chd->hrc", heads_of(queries), heads_of(keys), preferred_element_type=F32
    ) * HEAD ** (-0.5)
    if valid is not None:
        scores = jnp.where(valid[None, None, :], scores, -1e30)
    return scores


def attend_forward(queries, keys, values, valid):
    scores = scores_of(queries, keys, valid)
    top = jnp.max(scores, axis=-1, keepdims=True)
    expon = jnp.exp(scores - top)
    total = jnp.sum(expon, axis=-1, keepdims=True)
    mixed = jnp.einsum(
        "hrc,chd->rhd", to_low(expon / total), heads_of(values), preferred_element_type=F32
    )
    return to_low(mixed.reshape(queries.shape)), top + jnp.log(total)


def attend_backward(queries, keys, values, valid, log_total, delta_mixed):
    probs = jnp.exp(scores_of(queries, keys, valid) - log_total)
    delta_heads = heads_of(delta_mixed)
    delta_values = jnp.einsum("hrc,rhd->chd", to_low(probs), delta_heads, preferred_element_type=F32)
    delta_probs = jnp.einsum("rhd,chd->hrc", delta_heads, heads_of(values), preferred_element_type=F32)
    row_delta = jnp.sum(delta_probs * probs, axis=-1, keepdims=True)
    score_low = to_low(probs * (delta_probs - row_delta))
    scale = HEAD ** (-0.5)
    delta_query = jnp.einsum("hrc,chd->rhd", score_low, heads_of(keys), preferred_element_type=F32) * scale
    delta_keys = jnp.einsum("hrc,rhd->chd", score_low, heads_of(queries), preferred_element_type=F32) * scale
    return (
        to_low(delta_query.reshape(queries.shape)),
        to_low(delta_keys.reshape(keys.shape)),
        to_low(delta_values.reshape(keys.shape)),
    )


def body(
    custom,
    tokens,
    memory,
    lengths,
    tokens_cotangent,
    memory_cotangent,
    projections,
    output_maps,
    expand_weight,
    shrink_weight,
    projection_bias,
    norm_gain,
    norm_bias,
    expand_bias,
    shrink_bias,
):
    share = lax.axis_index("mem")
    chips = lax.axis_size("seq")
    width = tokens.shape[1]
    hidden = expand_weight.shape[1]
    part = projections.shape[1]
    rows = 2 * part

    def block(values, axis):
        low = to_low(values)
        wide = axis + 1
        return join(half(low, share, wide), swap(half(low, 1 - share, wide)), axis)

    vectors = jnp.concatenate(
        [projection_bias, norm_gain, norm_bias, shrink_bias[None], expand_bias.reshape(-1, part)]
    )
    count = vectors.shape[0]
    vec = to_low(jnp.pad(vectors.reshape(-1), (0, 1024 - vectors.size)).reshape(8, 128))
    blocks = (
        block(projections, 1),
        block(output_maps, 1),
        block(expand_weight, 0),
        block(shrink_weight, 0),
        both(vec),
    )
    if custom:
        proj_all, maps_all, expand_mat, shrink_mat, vec_all = gather_chips(chips // 4, blocks)
        proj_all = proj_all.reshape(6, width, width // 2)
        maps_all = maps_all.reshape(2, width, width)
        expand_mat = expand_mat.reshape(width, hidden)
        shrink_mat = shrink_mat.reshape(hidden, width)
    else:
        gather = lambda values, axis: lax.all_gather(values, "seq", axis=axis, tiled=True)
        proj_all = gather(blocks[0], 1)
        maps_all = both(gather(blocks[1], 1), 2)
        expand_mat = both(gather(blocks[2], 0), 1)
        shrink_mat = both(gather(blocks[3], 0), 1)
        vec_all = gather(blocks[4], 0)
    vec_all = vec_all.reshape(2 * chips, 1024)[:, : vectors.size].astype(F32)
    vec_all = vec_all.reshape(2 * chips, count, part).transpose(1, 0, 2).reshape(count, width)
    biases, gains, shifts, shrink_shift = vec_all[0:6], vec_all[6:9], vec_all[9:12], vec_all[12]
    expand_shift = vec_all[13:].reshape(-1, 2 * chips, part).transpose(1, 0, 2).reshape(hidden)
    bias_half = half(biases, share, 1)

    own_count = tokens.shape[0]
    length = lengths[0]
    own_valid = share * own_count + jnp.arange(own_count) < length
    all_valid = jnp.arange(2 * own_count) < length
    inputs, rows_all, memory_cot = both(tokens), both(memory), both(memory_cotangent)

    pack_query = to_low(matmul(rows_all, proj_all[0]) + bias_half[0])
    pack_keys = to_low(matmul(inputs, proj_all[1]))
    pack_values = to_low(matmul(inputs, proj_all[2]) + bias_half[1])
    pack_own, pack_total = attend_forward(pack_query, pack_keys, pack_values, all_valid)
    pack_mixed = both(pack_own, 1)
    packed = matmul(pack_mixed, maps_all[0]) + biases[2]
    packed_low = to_low(packed)
    memory_sum = rows_all.astype(F32) + packed
    new_memory = norm_apply(half(memory_sum, share, 0), gains[0], shifts[0])
    unpack_keys = to_low(matmul(packed_low, proj_all[4]))
    unpack_values = to_low(matmul(packed_low, proj_all[5]) + bias_half[4])
    unpack_query = to_low(matmul(inputs, proj_all[3]) + bias_half[3])
    unpack_own, unpack_total = attend_forward(unpack_query, unpack_keys, unpack_values, None)
    unpack_mixed = both(unpack_own, 1)
    middle_sum = tokens.astype(F32) + matmul(half(unpack_mixed, share, 0), maps_all[1]) + biases[5]
    middle = norm_apply(middle_sum, gains[1], shifts[1])
    middle_low = to_low(middle)
    hidden_in = matmul(middle_low, expand_mat) + expand_shift
    hidden_low = to_low(gelu_exact(hidden_in))
    output_sum = middle + matmul(hidden_low, shrink_mat) + shrink_shift
    layer_out = norm_apply(output_sum, gains[2], shifts[2])
    new_tokens = jnp.where(own_valid[:, None], layer_out, 0.0)

    delta_out = jnp.where(own_valid[:, None], tokens_cotangent.astype(F32), 0.0)
    dropped, norm_back = jax.vjp(norm_apply, output_sum, gains[2], shifts[2])
    delta_sum2, delta_gain2, delta_shift2 = norm_back(delta_out)
    delta_branch = to_low(delta_sum2)
    delta_hidden = matmul_right(delta_branch, shrink_mat)
    dropped, gelu_back = jax.vjp(gelu_exact, hidden_in)
    delta_hidden_in = to_low(gelu_back(delta_hidden)[0])
    delta_shrink = matmul_left(
        both(hidden_low), join(half(delta_branch, share, 1), swap(half(delta_branch, 1 - share, 1)))
    )
    delta_expand = matmul_left(
        both(middle_low), join(half(delta_hidden_in, share, 1), swap(half(delta_hidden_in, 1 - share, 1)))
    )
    delta_middle = delta_sum2 + matmul_right(delta_hidden_in, expand_mat)
    dropped, norm_back = jax.vjp(norm_apply, middle_sum, gains[1], shifts[1])
    delta_sum1, delta_gain1, delta_shift1 = norm_back(delta_middle)
    delta_own = to_low(delta_sum1)
    delta_unpacked = both(delta_own)
    delta_map1 = matmul_left(unpack_mixed, half(delta_unpacked, share, 1))
    delta_mixed = to_low(matmul_right(delta_unpacked, half(maps_all[1], share, 0)))
    delta_uquery, delta_ukeys, delta_uvalues = attend_backward(
        unpack_query, unpack_keys, unpack_values, None, unpack_total, delta_mixed
    )
    delta_proj3 = matmul_left(inputs, delta_uquery)
    delta_proj4 = matmul_left(packed_low, delta_ukeys)
    delta_proj5 = matmul_left(packed_low, delta_uvalues)
    partial = matmul_right(delta_ukeys, proj_all[4]) + matmul_right(delta_uvalues, proj_all[5])
    dropped, norm_back = jax.vjp(norm_apply, memory_sum, gains[0], shifts[0])
    delta_sum0 = norm_back(memory_cot.astype(F32))[0]
    dropped, norm_back = jax.vjp(norm_apply, half(memory_sum, share, 0), gains[0], shifts[0])
    dropped, delta_gain0, delta_shift0 = norm_back(memory_cotangent.astype(F32))
    delta_packed = to_low(delta_sum0 + (partial + swap(partial)))
    delta_map0 = matmul_left(pack_mixed, half(delta_packed, share, 1))
    delta_mixed = to_low(matmul_right(delta_packed, half(maps_all[0], share, 0)))
    delta_pquery, delta_pkeys, delta_pvalues = attend_backward(
        pack_query, pack_keys, pack_values, all_valid, pack_total, delta_mixed
    )
    delta_proj0 = matmul_left(rows_all, delta_pquery)
    delta_proj1 = matmul_left(inputs, delta_pkeys)
    delta_proj2 = matmul_left(inputs, delta_pvalues)
    partial = matmul_right(delta_pquery, proj_all[0])
    memory_grad = half(delta_sum0, share, 0) + half(partial, share, 0) + swap(half(partial, 1 - share, 0))
    partial = (
        matmul_right(delta_uquery, proj_all[3])
        + matmul_right(delta_pkeys, proj_all[1])
        + matmul_right(delta_pvalues, proj_all[2])
    )
    tokens_grad = delta_sum1 + half(partial, share, 0) + swap(half(partial, 1 - share, 0))

    zero = jnp.zeros((1, width // 2), F32)

    def spread(values):
        return join(values, zero[0])

    bias_grads = [
        spread(column_sum(delta_pquery)),
        spread(column_sum(delta_pvalues)),
        column_sum(half(delta_packed, share, 0)),
        spread(column_sum(delta_uquery)),
        spread(column_sum(delta_uvalues)),
        column_sum(delta_own),
    ]
    vec_grads = jnp.stack(
        bias_grads
        + [delta_gain0, delta_gain1, delta_gain2, delta_shift0, delta_shift1, delta_shift2, column_sum(delta_branch)]
    )
    vec_grads = vec_grads.reshape(13, 2 * chips, part).transpose(1, 0, 2).reshape(2 * chips, 13 * part)
    vec_grads = jnp.concatenate([vec_grads, column_sum(delta_hidden_in).reshape(2 * chips, -1)], axis=1)
    vec_grads = jnp.pad(vec_grads, ((0, 0), (0, 1024 - vec_grads.shape[1])))
    grads = (
        [delta_proj0, delta_proj1, delta_proj2, delta_proj3, delta_proj4, delta_proj5],
        [delta_map0, delta_map1],
    )
    if custom:
        grid = (chips // 4, 2, 2)
        proj_o, maps_o, expand_o, shrink_o, vec_o = reduce_chips(
            chips // 4,
            (
                jnp.stack([to_low(g) for g in grads[0]]).reshape((6,) + grid + (rows, width // 2)),
                jnp.stack([to_low(g) for g in grads[1]]).reshape((2,) + grid + (rows, width // 2)),
                to_low(delta_expand).reshape(grid + (rows, hidden // 2)),
                to_low(delta_shrink).reshape(grid + (hidden // chips, width // 2)),
                vec_grads.reshape(grid + (16, 128)),
            ),
        )
    else:
        reduce = lambda values, axis: lax.psum_scatter(values, "seq", scatter_dimension=axis, tiled=True)

        def finish(values, axis):
            return join(half(values, share, axis), swap(half(values, 1 - share, axis)), axis + 1)

        proj_o = finish(reduce(jnp.stack(grads[0]), 1), 1)
        maps_o = finish(reduce(jnp.stack(grads[1]), 1), 1)
        expand_o = finish(reduce(delta_expand, 0), 0)
        shrink_o = finish(reduce(delta_shrink, 0), 0)
        vec_o = lax.psum_scatter(vec_grads, AXES, scatter_dimension=0, tiled=True)
    vec_o = vec_o.reshape(-1)
    small = vec_o[: 13 * part].reshape(13, part)
    return (
        new_tokens,
        new_memory,
        tokens_grad,
        memory_grad,
        proj_o,
        maps_o,
        expand_o,
        shrink_o,
        small[0:6],
        small[6:9],
        small[9:12],
        vec_o[13 * part : 13 * part + hidden // (2 * chips)],
        small[12],
    )


def solution(mesh):
    rows, stacked = P(AXES, None), P(None, AXES, None)
    table, line = P(None, AXES), P(AXES)
    custom = mesh.shape["seq"] == 16 and mesh.shape["mem"] == 2
    return jax.shard_map(
        functools.partial(body, custom),
        mesh=mesh,
        in_specs=(rows, rows, P("seq"), rows, rows, stacked, stacked, rows, rows, table, table, table, line, line),
        out_specs=(rows, rows, rows, rows, stacked, stacked, rows, rows, table, table, table, line, line),
        check_vma=False,
    )
```

time: 1080 us -> 448 us (0.41)
  waiting for transfers between devices: 635 us -> 0.05 us
  Pallas kernels: 0 us -> 223 us
  blocking collectives: 199 us -> 0 us
  matrix products: 146 us -> 115 us
  other arithmetic: 23.6 us -> 45.4 us
  between operations: 16.4 us -> 3.31 us
    reduce_scatter x8 -> x0, waiting for transfers between devices: 532 us -> none  [the longest x1 142 us: body(): lax.psum_scatter(delta_expand, ('seq', 'mem'), scatter_dimension=0, tiled...]
    pallas_call x0 -> x2, Pallas kernels: none -> 223 us  [the longest x1 119 us: reduce_chips(): pl.pallas_call(functools.partial(reduce_kernel, far_count), out_shape=[ja...]
    all_gather x5 -> x0, blocking collectives: 119 us -> none  [the longest x1 39.4 us: body(): lax.all_gather(to_low(projection_bias), ('seq', 'mem'), axis=1, tiled=True)]
    all_gather x6 -> x0, waiting for transfers between devices: 103 us -> none  [the longest x1 77.7 us: body(): lax.all_gather(to_low(projections), ('seq', 'mem'), axis=1, tiled=True)]
    unnamed x2 -> x0, blocking collectives: 80.1 us -> none
    dot_general x20, matrix products: 71 us -> 56.5 us  [the longest x10 39.3 us: matmul(): return jnp.dot(left, right, preferred_element_type=F32)]
    another operation x8 -> x15, local copies, waits for them, and re-layouts: 20.8 us -> 7.91 us  [the longest x14 5.95 us: body(): jnp.stack(bias_grads + [delta_gain0, delta_gain1, delta_gain2, delta_shif...]
  transfers between devices with their start and end apart: 14 -> 18, of which waited for: 9 -> 0; matrix products, arithmetic and copies ran while one was open for 12% -> 33% of each run, Pallas kernels for 0% -> 51%
where the time goes in v1:
time: 448 us; the launch traced here: 440 us
  Pallas kernels  223 us (50%)
  matrix products  115 us (26%)
  local copies, waits for them, and re-layouts  47.2 us (11%)
  other arithmetic  45.4 us (10%)
  starting transfers between devices  5.5 us (1%)
    pallas_call x1, Pallas kernels, reduce_chips(): pl.pallas_call(functools.partial(reduce_kernel, far_count), out_shape=[ja...  119 us
    pallas_call x1, Pallas kernels, gather_chips(): pl.pallas_call(functools.partial(gather_kernel, far_count), out_shape=[ja...  105 us
    dot_general x10, matrix products, matmul(): return jnp.dot(left, right, preferred_element_type=F32)  39.3 us
    dot_general x10, matrix products, matmul_left(): lax.dot_general(left, right, (((0,), (0,)), ((), ())), preferred_element_...  31.8 us
    dot_general x10, matrix products, matmul_right(): lax.dot_general(left, right, (((1,), (1,)), ((), ())), preferred_element_...  23.4 us
    unnamed x194, local copies, waits for them, and re-layouts  15.1 us
    convert_element_type x8, other arithmetic, to_low(): return values.astype(LOW)  11.2 us
  transfers between devices with their start and end apart: 18, of which 0 were waited for; matrix products, arithmetic and copies ran while one was open for 33% of the time, Pallas kernels for 51%

profile of v1, /device:TPU:0, one launch (start us, length us, event | category | flops | bytes accessed | tf_op | source)
XLA Modules:
  0.0 439.7 jit_solution(14514149456698033944)
XLA Ops:
  0.7 1.0 convert_element_type.246
  4.9 1.0 convert_element_type.249
  15.4 104.7 %gather_weights.1 = (bf16[6,4,2,2,48,384]{5,4,3,2,1,0:T(8,128)(2,1)}, bf16[2,4,2,2,48,768]{5,4,3,2,1,0:T(8,128)(2,1)}, bf16[4,2,2,48,3072]{4,3,2,1,0:T(8,128)(2,...) custom-call(bf16[6,48,384]{2,1,0:T(8,128)(2,1)} %maximum_select_fusion.16.proj, ...), custom_call_target="tpu_custom_call" | custom-call | tf_op jit(solution)/shard_map/gather_weights/pallas_call | solution.py:242
  123.8 2.5 fusion.86
  126.5 1.8 fusion.87
  129.0 1.4 fusion.48
  130.6 2.8 convolution_convert_fusion.2
  133.4 1.1 fusion.90
  134.5 1.4 fusion.13
  136.2 2.9 add_convert_fusion.2
  139.2 1.9 fusion.53
  142.0 2.8 add_convert_fusion.1
  144.9 1.9 fusion.82
  146.8 1.0 fusion.49
  147.8 1.7 copy.109
  150.1 1.0 multiply_reduce_fusion.2
  151.2 1.1 fusion.14
  152.3 1.5 copy-done.10
  153.8 1.4 fusion.41
  155.7 1.7 multiply_reduce_fusion.10
  157.5 2.4 fusion.81
  162.2 1.2 fusion.45
  164.1 20.4 %multiply_convert_fusion.2 = (bf16[512,3072]{1,0:T(8,128)(2,1)}, f32[512,3072]{1,0:T(8,128)}, f32[512,3072]{1,0:T(8,128)}) fusion(f32[3072]{0:T(1024)S(1)} %add.311, bf16[512,768]{1,0:T(8,128)(2,1)} %fusion.45, bf16[768,3072]{1,0:T(8,128)(2,1)S(1)} %bitcast.204), kind=kOutput, calls=%fused_computation.17 | convolution fusion | flops 2519728128 | bytes 21245952 | tf_op jit(solution)/shard_map/dot_general | solution.py:19
  184.5 4.8 %fusion.92 = (f32[512]{0:T(512)S(1)}, f32[512,768]{1,0:T(8,128)S(1)}) fusion(f32[768]{0:T(1024)S(1)} %add.315, bf16[512,3072]{1,0:T(8,128)(2,1)} %get-tuple-element.63, bf16[3072,768]{1,0:T(8,128)(2,1)S(1)} %bitcast.209, f32[768]{0:T(1024)S(1)} %add.308, f32[768]{0:T(1024)S(1)} %mul.311, f32[512]{0:T(512)S(1)} %fusion.71, ...), kind=kOutput, calls=%fused_computation.252 | convolution fusion | flops 2418671104 | bytes 11025408 | tf_op jit(solution)/shard_map/dot_general | solution.py:19
  190.4 2.0 fusion.84
  192.6 9.2 %convert_reduce_fusion = (f32[3072]{0:T(1024)}, bf16[512,3072]{1,0:T(8,128)(2,1)S(1)}) fusion(f32[512,3072]{1,0:T(8,128)} %get-tuple-element.64, f32[512,3072]{1,0:T(8,128)} %get-tuple-element.108, f32[3072]{0:T(1024)S(1)} %add.311, bf16[512,768]{1,0:T(8,128)(2,1)S(1)} %get-tuple-element.48, bf16[3072,768]{1,0:T(8,128)(2,1)} %bitcast.206), kind=kOutput, calls=%fused_computation.9 | convolution fusion | flops 2442654720 | bytes 21258240 | tf_op jit(solution)/shard_map/dot_general | solution.py:27
  201.8 3.7 multiply_reduce_fusion.4
  206.2 1.3 convert_reduce_fusion.2
  209.1 1.9 constant_dynamic-slice_fusion.4
  214.0 1.4 stack.89
  217.5 2.4 maximum_select_fusion.8
  219.9 2.4 convolution_convert_fusion.1
  222.3 2.0 multiply_reduce_fusion.1
  224.3 1.9 convert_reduce_fusion.6
  226.2 1.8 multiply_convert_fusion.1
  228.0 2.3 fusion.46
  231.5 1.2 convolution_convert_fusion.6
  232.8 1.9 convolution_convert_fusion.3
  234.6 1.2 convolution_convert_fusion.5
  238.0 3.8 fusion.93
  241.8 3.8 convolution_convert_fusion.7
  245.6 2.6 add_convert_fusion.5
  248.2 1.1 convolution_convert_fusion.11
  249.3 1.7 copy.127
  251.0 5.0 %multiply_reduce_fusion = (f32[6,256]{1,0:T(8,128)S(1)}, f32[6,256,1024]{2,1,0:T(8,128)S(1)}) fusion(f32[6,256,1024]{2,1,0:T(8,128)} %copy-done.9, f32[6,256]{1,0:T(8,128)S(1)} %log_add_fusion.1, bf16[256,6,64]{0,2,1:T(8,128)(2,1)} %bitcast.181, bf16[1024,6,64]{0,2,1:T(8,128)(2,1)} %bitcast.188), kind=kOutput, calls=%fused_computation.11 | convolution fusion | flops 206043648 | bytes 13578240 | tf_op jit(solution)/shard_map/rhd,chd->hrc/dot_general | solution.py:519
  256.1 1.2 convert_reduce_fusion.4
  257.3 1.6 multiply_convert_fusion
  260.1 1.2 convert_reduce_fusion.8
  261.5 1.0 fusion.95
  263.3 1.0 add_add_fusion
  264.4 1.3 constant_dynamic-slice_fusion.6
  268.3 1.8 convert_reduce_fusion.5
  271.3 3.0 convolution_convert_fusion.9
  275.2 2.5 convolution_convert_fusion.8
  280.4 1.2 convolution_convert_fusion.4
  281.9 5.9 %convolution_convert_fusion = bf16[768,1536]{1,0:T(8,128)(2,1)S(1)} fusion(bf16[512,1536]{1,0:T(8,128)(2,1)} %collective-permute-done.15, bf16[512,1536]{1,0:T(8,128)(2,1)S(1)} %copy-done.46, pred[]{:T(512)S(6)} %eq.2, bf16[512,768]{1,0:T(8,128)(2,1)} %collective-permute-done.14, bf16[512,768]{1,0:T(8,128)(2,1)} %fusion.45), kind=kOutput, calls=%fused_computation.43 | convolution fusion | flops 2438332416 | bytes 7077889 | tf_op jit(solution)/shard_map/dot_general | solution.py:23
  288.7 1.4 pad_maximum_fusion.maps
  290.0 1.5 select_maximum_fusion
  291.6 1.6 reshape.379.vec
  293.2 2.0 constant_dynamic-update-slice_fusion.proj
  295.1 2.0 add_add_fusion.8
  297.2 10.6 %fusion.16 = bf16[3072,384]{1,0:T(8,128)(2,1)} fusion(bf16[512,3072]{1,0:T(8,128)(2,1)} %collective-permute-done.16, bf16[512,3072]{1,0:T(8,128)(2,1)} %get-tuple-element.63, pred[]{:T(512)S(6)} %eq.2, bf16[512,384]{1,0:T(8,128)(2,1)} %collective-permute-done.17, bf16[512,384]{1,0:T(8,128)(2,1)} %get-tuple-element.77), kind=kOutput, calls=%fused_computation.41 | convolution fusion | flops 2448949248 | bytes 9437185 | tf_op jit(solution)/shard_map/dot_general | solution.py:23
  307.8 118.7 %sum_gradients.1 = (f32[6,24,768]{2,1,0:T(8,128)S(1)}, f32[2,24,768]{2,1,0:T(8,128)S(1)}, f32[24,3072]{1,0:T(8,128)S(1)}, f32[96,768]{1,0:T(8,128)S(1)}, f32[8,128]{1,0:T(8,128)S(1)}) custom-call(bf16[6,4,2,2,48,384]{5,4,3,2,1,0:T(8,128)(2,1)} %constant_dynamic-update-slice_fusion.proj, bf16[2,4,2,2,48,384]{5,4,3,2,1,0:T(8,128)(2,1)S(1)} %pad_maximum_fusion.maps, ...), custom_call_target="tpu_custom_call" | custom-call | tf_op jit(solution)/shard_map/sum_gradients/pallas_call | solution.py:450
  432.6 3.9 add_add_fusion.3
  (350 shorter events, 52.9 us)
Async XLA Ops:
  1.7 12.9 %collective-permute-start.1 = (bf16[6,24,384]{2,1,0:T(8,128)(2,1)S(1)}, bf16[6,24,384]{2,1,0:T(8,128)(2,1)S(1)}, u32[]{:S(2)}, u32[]{:S(2)}) collective-permute-start(bf16[6,24,384]{2,1,0:T(8,128)(2,1)S(1)} %get-tuple-element.81), channel_id=1, source_target_pairs={{0,1},{1,0},{2,3},{3,2},{4,5},{5,4},{6,7},{7,6},{8,9},{9,8},{10,11... | collective-permute-start | bytes 331784 | tf_op jit(solution)/shard_map/ppermute | solution.py:39
  3.2 8.9 %collective-permute-start.2 = (bf16[2,24,384]{2,1,0:T(8,128)(2,1)S(1)}, bf16[2,24,384]{2,1,0:T(8,128)(2,1)S(1)}, u32[]{:S(2)}, u32[]{:S(2)}) collective-permute-start(bf16[2,24,384]{2,1,0:T(8,128)(2,1)S(1)} %get-tuple-element.96), channel_id=1, source_target_pairs={{0,1},{1,0},{2,3},{3,2},{4,5},{5,4},{6,7},{7,6},{8,9},{9,8},{10,11... | collective-permute-start | bytes 110600 | tf_op jit(solution)/shard_map/ppermute | solution.py:39
  4.3 8.9 %collective-permute-start.3 = (bf16[24,1536]{1,0:T(8,128)(2,1)S(1)}, bf16[24,1536]{1,0:T(8,128)(2,1)S(1)}, u32[]{:S(2)}, u32[]{:S(2)}) collective-permute-start(bf16[24,1536]{1,0:T(8,128)(2,1)S(1)} %get-tuple-element.94), channel_id=1, source_target_pairs={{0,1},{1,0},{2,3},{3,2},{4,5},{5,4},{6,7},{7,6},{8,9},{9,8},{10,11... | collective-permute-start | bytes 221192 | tf_op jit(solution)/shard_map/ppermute | solution.py:39
  5.9 8.1 %collective-permute-start.4 = (bf16[96,384]{1,0:T(8,128)(2,1)S(1)}, bf16[96,384]{1,0:T(8,128)(2,1)S(1)}, u32[]{:S(2)}, u32[]{:S(2)}) collective-permute-start(bf16[96,384]{1,0:T(8,128)(2,1)S(1)} %get-tuple-element.92), channel_id=1, source_target_pairs={{0,1},{1,0},{2,3},{3,2},{4,5},{5,4},{6,7},{7,6},{8,9},{9,8},{10,11... | collective-permute-start | bytes 221192 | tf_op jit(solution)/shard_map/ppermute | solution.py:39
  9.7 1.7 collective-permute-start.5
  11.5 116.9 %collective-permute-start.6 = (bf16[128,768]{1,0:T(8,128)(2,1)}, bf16[128,768]{1,0:T(8,128)(2,1)S(1)}, u32[]{:S(2)}, u32[]{:S(2)}) collective-permute-start(bf16[128,768]{1,0:T(8,128)(2,1)} %param.15), channel_id=1, source_target_pairs={{0,1},{1,0},{2,3},{3,2},{4,5},{5,4},{6,7},{7,6},{8,9},{9,8},{10,11... | collective-permute-start | bytes 589832 | tf_op jit(solution)/shard_map/ppermute | solution.py:39
  12.1 118.4 %collective-permute-start = (bf16[512,768]{1,0:T(8,128)(2,1)}, bf16[512,768]{1,0:T(8,128)(2,1)}, u32[]{:S(2)}, u32[]{:S(2)}) collective-permute-start(bf16[512,768]{1,0:T(8,128)(2,1)} %param.14), channel_id=1, source_target_pairs={{0,1},{1,0},{2,3},{3,2},{4,5},{5,4},{6,7},{7,6},{8,9},{9,8},{10,11... | collective-permute-start | bytes 2359304 | tf_op jit(solution)/shard_map/ppermute | solution.py:39
  13.2 142.5 %collective-permute-start.10 = (bf16[128,768]{1,0:T(8,128)(2,1)}, bf16[128,768]{1,0:T(8,128)(2,1)}, u32[]{:S(2)}, u32[]{:S(2)}) collective-permute-start(bf16[128,768]{1,0:T(8,128)(2,1)} %param.18), channel_id=1, source_target_pairs={{0,1},{1,0},{2,3},{3,2},{4,5},{5,4},{6,7},{7,6},{8,9},{9,8},{10,11... | collective-permute-start | bytes 589832 | tf_op jit(solution)/shard_map/ppermute | solution.py:39
  126.3 4.3 copy-start.29
  126.3 9.7 %copy-start.36 = (bf16[1,4,2,2,48,384]{5,4,3,2,1,0:T(8,128)(2,1)}, bf16[1,4,2,2,48,384]{5,4,3,2,1,0:T(8,128)(2,1)S(1)}, u32[]{:S(2)}) copy-start(bf16[1,4,2,2,48,384]{5,4,3,2,1,0:T(8,128)(2,1)S(1)} %get-tuple-element.70) | copy-start | bytes 1769476
  126.3 15.7 %copy-start.31 = (bf16[1,4,2,2,48,384]{5,4,3,2,1,0:T(8,128)(2,1)}, bf16[1,4,2,2,48,384]{5,4,3,2,1,0:T(8,128)(2,1)S(1)}, u32[]{:S(2)}) copy-start(bf16[1,4,2,2,48,384]{5,4,3,2,1,0:T(8,128)(2,1)S(1)} %get-tuple-element.66) | copy-start | bytes 1769476
  126.3 20.5 %copy-start.16 = (bf16[1,4,2,2,48,384]{5,4,3,2,1,0:T(8,128)(2,1)}, bf16[1,4,2,2,48,384]{5,4,3,2,1,0:T(8,128)(2,1)S(1)}, u32[]{:S(2)}) copy-start(bf16[1,4,2,2,48,384]{5,4,3,2,1,0:T(8,128)(2,1)S(1)} %get-tuple-element.67) | copy-start | bytes 1769476
  126.3 23.3 %copy-start.14 = (bf16[1,4,2,2,48,384]{5,4,3,2,1,0:T(8,128)(2,1)}, bf16[1,4,2,2,48,384]{5,4,3,2,1,0:T(8,128)(2,1)S(1)}, u32[]{:S(2)}) copy-start(bf16[1,4,2,2,48,384]{5,4,3,2,1,0:T(8,128)(2,1)S(1)} %get-tuple-element.65) | copy-start | bytes 1769476
  134.5 4.7 %copy-start.9 = (f32[6,256,1024]{2,1,0:T(8,128)}, f32[6,256,1024]{2,1,0:T(8,128)S(1)}, u32[]{:S(2)}) copy-start(f32[6,256,1024]{2,1,0:T(8,128)S(1)} %get-tuple-element.102) | copy-start | bytes 18874372
  141.3 3.5 copy-start.52
  141.3 3.5 collective-permute-start.7
  144.8 5.3 %copy-start.21 = (bf16[1024,384]{0,1:T(8,128)(2,1)}, bf16[1024,384]{0,1:T(8,128)(2,1)S(1)}, u32[]{:S(2)}) copy-start(bf16[1024,384]{0,1:T(8,128)(2,1)S(1)} %add_convert_fusion.1) | copy-start | bytes 2359300
  155.6 4.9 %collective-permute-start.8 = (bf16[1024,384]{1,0:T(8,128)(2,1)S(1)}, bf16[1024,384]{1,0:T(8,128)(2,1)S(1)}, u32[]{:S(2)}, u32[]{:S(2)}) collective-permute-start(bf16[1024,384]{1,0:T(8,128)(2,1)S(1)} %copy.113), channel_id=1, source_target_pairs={{0,1},{1,0},{2,3},{3,2},{4,5},{5,4},{6,7},{7,6},{8,9},{9,8},{10,11... | collective-permute-start | bytes 2359304 | tf_op jit(solution)/shard_map/ppermute | solution.py:39
  155.7 5.2 %copy-start.47 = (bf16[1,4,2,2,48,768]{5,4,3,2,1,0:T(8,128)(2,1)S(1)}, bf16[1,4,2,2,48,768]{5,4,3,2,1,0:T(8,128)(2,1)}, u32[]{:S(2)}) copy-start(bf16[1,4,2,2,48,768]{5,4,3,2,1,0:T(8,128)(2,1)} %get-tuple-element.74) | copy-start | bytes 3538948
  155.7 5.2 %copy-start.68 = (bf16[512,768]{1,0:T(8,128)(2,1)S(1)}, bf16[512,768]{1,0:T(8,128)(2,1)}, u32[]{:S(2)}) copy-start(bf16[512,768]{1,0:T(8,128)(2,1)} %param.14) | copy-start | bytes 2359300
  160.9 3.1 slice-start.5
  161.8 22.6 %slice-start.6 = ((s8[4718592]{0:T(1024)(128)(4,1)}), s8[4194304]{0:T(1024)(128)(4,1)S(1)}, s32[]{:S(2)}) async-start(s8[4718592]{0:T(1024)(128)(4,1)} %bitcast.207), calls=%async_computation.6 | async-start | bytes 8388608
  164.0 20.4 %slice-start.7 = ((s8[4718592]{0:T(1024)(128)(4,1)}), s8[524288]{0:T(1024)(128)(4,1)S(1)}, s32[]{:S(2)}) async-start(s8[4718592]{0:T(1024)(128)(4,1)} %bitcast.207), calls=%async_computation.7 | async-start | bytes 1048576
  184.4 5.1 %copy-start.23 = (bf16[512,768]{1,0:T(8,128)(2,1)S(1)}, bf16[512,768]{1,0:T(8,128)(2,1)}, u32[]{:S(2)}) copy-start(bf16[512,768]{1,0:T(8,128)(2,1)} %param.17) | copy-start | bytes 2359300
  184.5 5.1 %copy-start.65 = (pred[512]{0:T(512)(128)(4,1)S(1)}, pred[512]{0:T(512)(128)(4,1)}, u32[]{:S(2)}) copy-start(pred[512]{0:T(512)(128)(4,1)} %add_compare_fusion) | copy-start | bytes 1540
  207.5 10.0 %collective-permute-start.9 = (bf16[512,768]{1,0:T(8,128)(2,1)}, bf16[512,768]{1,0:T(8,128)(2,1)}, u32[]{:S(2)}, u32[]{:S(2)}) collective-permute-start(bf16[512,768]{1,0:T(8,128)(2,1)} %get-tuple-element.50), channel_id=1, source_target_pairs={{0,1},{1,0},{2,3},{3,2},{4,5},{5,4},{6,7},{7,6},{8,9},{9,8},{10,11... | collective-permute-start | bytes 2359304 | tf_op jit(solution)/shard_map/ppermute | solution.py:39
  208.5 73.2 %collective-permute-start.14 = (bf16[512,768]{1,0:T(8,128)(2,1)}, bf16[512,768]{1,0:T(8,128)(2,1)}, u32[]{:S(2)}, u32[]{:S(2)}) collective-permute-start(bf16[512,768]{1,0:T(8,128)(2,1)} %fusion.45), channel_id=1, source_target_pairs={{0,1},{1,0},{2,3},{3,2},{4,5},{5,4},{6,7},{7,6},{8,9},{9,8},{10,11... | collective-permute-start | bytes 2359304 | tf_op jit(solution)/shard_map/ppermute | solution.py:39
  208.6 88.6 %collective-permute-start.16 = (bf16[512,3072]{1,0:T(8,128)(2,1)}, bf16[512,3072]{1,0:T(8,128)(2,1)}, u32[]{:S(2)}, u32[]{:S(2)}) collective-permute-start(bf16[512,3072]{1,0:T(8,128)(2,1)} %get-tuple-element.63), channel_id=1, source_target_pairs={{0,1},{1,0},{2,3},{3,2},{4,5},{5,4},{6,7},{7,6},{8,9},{9,8},{10,11... | collective-permute-start | bytes 9437192 | tf_op jit(solution)/shard_map/ppermute | solution.py:39
  209.1 13.2 %slice-start.2 = ((s8[6291456]{0:T(1024)(128)(4,1)}), s8[2097152]{0:T(1024)(128)(4,1)S(1)}, s32[]{:S(2)}) async-start(s8[6291456]{0:T(1024)(128)(4,1)} %bitcast.142), calls=%async_computation.2 | async-start | bytes 4194304
  211.0 70.9 %collective-permute-start.15 = (bf16[512,1536]{1,0:T(8,128)(2,1)}, bf16[512,1536]{1,0:T(8,128)(2,1)}, u32[]{:S(2)}, u32[]{:S(2)}) collective-permute-start(bf16[512,1536]{1,0:T(8,128)(2,1)} %get-tuple-element.72), channel_id=1, source_target_pairs={{0,1},{1,0},{2,3},{3,2},{4,5},{5,4},{6,7},{7,6},{8,9},{9,8},{10,11... | collective-permute-start | bytes 4718600 | tf_op jit(solution)/shard_map/ppermute | solution.py:39
  212.1 85.1 %collective-permute-start.17 = (bf16[512,384]{1,0:T(8,128)(2,1)}, bf16[512,384]{1,0:T(8,128)(2,1)}, u32[]{:S(2)}, u32[]{:S(2)}) collective-permute-start(bf16[512,384]{1,0:T(8,128)(2,1)} %get-tuple-element.78), channel_id=1, source_target_pairs={{0,1},{1,0},{2,3},{3,2},{4,5},{5,4},{6,7},{7,6},{8,9},{9,8},{10,11... | collective-permute-start | bytes 1179656 | tf_op jit(solution)/shard_map/ppermute | solution.py:39
  217.5 4.8 %slice-start.3 = ((s8[6291456]{0:T(1024)(128)(4,1)}), s8[4194304]{0:T(1024)(128)(4,1)S(1)}, s32[]{:S(2)}) async-start(s8[6291456]{0:T(1024)(128)(4,1)} %bitcast.142), calls=%async_computation.3 | async-start | bytes 8388608
  228.0 3.1 copy-start.15
  231.5 3.1 copy-start.40
  232.8 3.1 copy-start.17
  236.3 9.3 %copy-start.24 = (f32[256,768]{1,0:T(8,128)}, f32[256,768]{1,0:T(8,128)S(1)}, u32[]{:S(2)}) copy-start(f32[256,768]{1,0:T(8,128)S(1)} %convolution_add_fusion) | copy-start | bytes 2359300
  236.3 9.3 %collective-permute-start.11 = (f32[256,768]{1,0:T(8,128)S(1)}, f32[256,768]{1,0:T(8,128)}, u32[]{:S(2)}, u32[]{:S(2)}) collective-permute-start(f32[256,768]{1,0:T(8,128)S(1)} %convolution_add_fusion), channel_id=1, source_target_pairs={{0,1},{1,0},{2,3},{3,2},{4,5},{5,4},{6,7},{7,6},{8,9},{9,8},{10,11... | collective-permute-start | bytes 2359304 | tf_op jit(solution)/shard_map/ppermute | solution.py:39
  241.8 3.8 copy-start.22
  241.8 3.8 copy-start.64
  245.6 10.5 %slice-start = ((s8[6291456]{0:T(1024)(128)(4,1)}), s8[2097152]{0:T(1024)(128)(4,1)S(1)}, s32[]{:S(2)}) async-start(s8[6291456]{0:T(1024)(128)(4,1)} %bitcast.140), calls=%async_computation | async-start | bytes 4194304
  251.0 5.0 %slice-start.1 = ((s8[6291456]{0:T(1024)(128)(4,1)}), s8[4194304]{0:T(1024)(128)(4,1)S(1)}, s32[]{:S(2)}) async-start(s8[6291456]{0:T(1024)(128)(4,1)} %bitcast.140), calls=%async_computation.1 | async-start | bytes 8388608
  251.0 5.0 %copy-start.41 = (bf16[256,384]{0,1:T(8,128)(2,1)S(1)}, bf16[256,384]{0,1:T(8,128)(2,1)}, u32[]{:S(2)}) copy-start(bf16[256,384]{0,1:T(8,128)(2,1)} %copy.127) | copy-start | bytes 589828
  257.3 5.2 %copy-start.25 = (bf16[6,64,1024]{2,1,0:T(8,128)(2,1)}, bf16[6,64,1024]{2,1,0:T(8,128)(2,1)S(1)}, u32[]{:S(2)}) copy-start(bf16[6,64,1024]{2,1,0:T(8,128)(2,1)S(1)} %get-tuple-element.119) | copy-start | bytes 2359300
  265.6 166.9 %collective-permute-start.12 = (f32[512,768]{1,0:T(8,128)}, f32[512,768]{1,0:T(8,128)}, u32[]{:S(2)}, u32[]{:S(2)}) collective-permute-start(f32[512,768]{1,0:T(8,128)} %constant_dynamic-slice_fusion.6), channel_id=1, source_target_pairs={{0,1},{1,0},{2,3},{3,2},{4,5},{5,4},{6,7},{7,6},{8,9},{9,8},{10,11... | collective-permute-start | bytes 4718600 | tf_op jit(solution)/shard_map/ppermute | solution.py:39
  266.1 5.0 %copy-start.59 = (f32[1,32,24]{2,1,0:T(8,128)S(1)}, f32[1,32,24]{2,1,0:T(8,128)}, u32[]{:S(2)}) copy-start(f32[1,32,24]{2,1,0:T(8,128)} %stack.85) | copy-start | bytes 9220
  266.1 5.0 %copy-start.60 = (f32[1,32,24]{2,1,0:T(8,128)S(1)}, f32[1,32,24]{2,1,0:T(8,128)}, u32[]{:S(2)}) copy-start(f32[1,32,24]{2,1,0:T(8,128)} %stack.86) | copy-start | bytes 9220
  266.1 5.1 %copy-start.58 = (f32[1,32,24]{2,1,0:T(8,128)S(1)}, f32[1,32,24]{2,1,0:T(8,128)}, u32[]{:S(2)}) copy-start(f32[1,32,24]{2,1,0:T(8,128)} %stack.87) | copy-start | bytes 9220
  266.1 5.1 %copy-start.57 = (f32[1,32,24]{2,1,0:T(8,128)S(1)}, f32[1,32,24]{2,1,0:T(8,128)}, u32[]{:S(2)}) copy-start(f32[1,32,24]{2,1,0:T(8,128)} %stack.89) | copy-start | bytes 9220
  266.1 5.1 %copy-start.56 = (f32[1,32,24]{2,1,0:T(8,128)S(1)}, f32[1,32,24]{2,1,0:T(8,128)}, u32[]{:S(2)}) copy-start(f32[1,32,24]{2,1,0:T(8,128)} %stack.90) | copy-start | bytes 9220
  266.5 7.8 %copy-start.20 = (f32[256,768]{1,0:T(8,128)}, f32[256,768]{1,0:T(8,128)S(1)}, u32[]{:S(2)}) copy-start(f32[256,768]{1,0:T(8,128)S(1)} %fusion.96) | copy-start | bytes 2359300
  266.5 4.7 %copy-start.54 = (f32[1,32,24]{2,1,0:T(8,128)S(1)}, f32[1,32,24]{2,1,0:T(8,128)}, u32[]{:S(2)}) copy-start(f32[1,32,24]{2,1,0:T(8,128)} %stack.92) | copy-start | bytes 9220
  266.5 4.7 %copy-start.55 = (f32[1,32,24]{2,1,0:T(8,128)S(1)}, f32[1,32,24]{2,1,0:T(8,128)}, u32[]{:S(2)}) copy-start(f32[1,32,24]{2,1,0:T(8,128)} %stack.93) | copy-start | bytes 9220
  271.3 4.0 copy-start.26
  271.3 4.0 copy-start.69
  275.2 3.5 copy-start.51
  275.2 4.3 copy-start.35
  277.8 4.1 copy-start.46
  281.7 13.4 %collective-permute-start.13 = (f32[128,768]{1,0:T(8,128)}, f32[128,768]{1,0:T(8,128)}, u32[]{:S(2)}, u32[]{:S(2)}) collective-permute-start(f32[128,768]{1,0:T(8,128)} %constant_dynamic-slice_fusion.5), channel_id=1, source_target_pairs={{0,1},{1,0},{2,3},{3,2},{4,5},{5,4},{6,7},{7,6},{8,9},{9,8},{10,11... | collective-permute-start | bytes 1179656 | tf_op jit(solution)/shard_map/ppermute | solution.py:39
  297.2 10.6 %copy-start = (f32[4,2,2,16,128]{4,3,2,1,0:T(8,128)S(1)}, f32[4,2,2,16,128]{4,3,2,1,0:T(8,128)}, u32[]{:S(2)}) copy-start(f32[4,2,2,16,128]{4,3,2,1,0:T(8,128)} %reshape.379.vec) | copy-start | bytes 393220
  307.8 124.8 %copy-start.62 = (f32[512]{0:T(512)S(1)}, f32[512]{0:T(512)}, u32[]{:S(2)}) copy-start(f32[512]{0:T(512)} %copy-done.61) | copy-start | bytes 6148
  432.5 3.9 copy-start.2
  432.5 4.7 %copy-start.8 = (f32[2,24,768]{2,1,0:T(8,128)S(1)}, f32[2,24,768]{2,1,0:T(8,128)}, u32[]{:S(2)}) copy-start(f32[2,24,768]{2,1,0:T(8,128)} %copy-done.7) | copy-start | bytes 442372
  432.5 5.3 %copy-start.6 = (f32[24,3072]{1,0:T(8,128)S(1)}, f32[24,3072]{1,0:T(8,128)}, u32[]{:S(2)}) copy-start(f32[24,3072]{1,0:T(8,128)} %copy-done.5) | copy-start | bytes 884740
  432.5 6.0 %copy-start.4 = (f32[96,768]{1,0:T(8,128)S(1)}, f32[96,768]{1,0:T(8,128)}, u32[]{:S(2)}) copy-start(f32[96,768]{1,0:T(8,128)} %copy-done.3) | copy-start | bytes 884740
  (40 other events, 82.0 us)
